TPU v7x, 512 devices: a whole 4x8x8 slice. The times are simulated.
512 devices in a mesh: side: 2 (over y_hi), grp: 8 (over z), dev: 32 (over x, y_lo, core).
Axes of the slice: x: 4, y: 8 (y_hi: 2, y_lo: 4; y = y_hi * 4 + y_lo), z: 8, core: 2. Of those that a mesh axis runs over, the one named last changes fastest.
Arguments:
- sources: float32 [2, 8, 65536], P('side', None, ('grp', 'dev')), may hold values from -2500 to 2500
- near_blocks: bfloat16 [2, 8192, 128, 128], P('side', ('grp', 'dev')), may hold values from -0.125 to 0.125
- block_rows: int32 [2, 8192], P('side', ('grp', 'dev')), may hold values from 0 to 1, as said below
- block_cols: int32 [2, 8192], P('side', ('grp', 'dev')), may hold values from 0 to 511, as said below
- mirror: int32 [65536], P(('grp', 'dev')), may hold values from 0 to 127, as said below
Outputs:
- krylov_basis: float32 [4, 2, 8, 65536], P(None, 'side', None, ('grp', 'dev'))
- hessenberg: float32 [8, 4, 3], replicated
Inputs may be any that keep to these rules, and one draw needn't show every extreme that they name: `block_rows`: in each device's aligned run of 32 entries, the first 2 are 0 to 1 in order. `block_cols`: in each device's aligned run of 32 entries, the first 2 name that device's own blocks in order, and every entry names a block of an owner at most 4 owners before or after that device (owners of a half counted in the order grp, dev); where such owners exist, some entry names a block of the owner 4 before and some one of the owner 4 after. `mirror`: each aligned run of 128 entries is a permutation of 0 to 127.
All inputs are finite; a program needn't handle non-finite values.
Results may differ from a plain program's by a relative error of at most 0.005.
Values may be sent and summed in bfloat16 or wider, within the bound.
A program may use at most 64 MiB of HBM per device.

v0:
```python
import jax
import jax.numpy as jnp
from jax import lax
from jax.sharding import PartitionSpec as P

BLOCK = 128
BLK_DEV = 2
WIN = 4
ITERS = 3


epsilon = 1e-06


def shifted(block, axis, distance):
    devices = range(lax.axis_size(axis))
    route = [(i - distance, i) for i in devices if i - distance in devices]
    return lax.ppermute(block, axis, route)


def swapped(value, axis, distance):
    return lax.ppermute(value, axis, [(i, i ^ 1 << distance) for i in range(lax.axis_size(axis))])


def on_device(sources, near_blocks, block_rows, block_cols, mirror):
    side_index = lax.axis_index("side")
    is_port = side_index == 0
    owner_index = lax.axis_index(("grp", "dev"))
    vectors = sources.shape[1]
    panels = sources.shape[2]
    total_panels = (
        1.0 * panels * lax.axis_size("side") * lax.axis_size("grp") * lax.axis_size("dev")
    )
    mirror_onehot = (
        mirror.reshape(BLK_DEV, BLOCK)[:, :, None]
        == jnp.arange(BLOCK, dtype=jnp.int32)[None, None, :]
    ).astype(jnp.float32)
    row_onehot = (block_rows[0][None, :] == jnp.arange(BLK_DEV, dtype=jnp.int32)[:, None]).astype(
        jnp.float32
    )
    window_cols = block_cols[0] - (owner_index - WIN) * BLK_DEV
    blocks = near_blocks[0]
    start = sources[0]
    inner_scale = 1.0 / total_panels
    squares = lax.psum(jnp.sum(start * start, axis=1), ("side", "grp", "dev"))
    length = jnp.sqrt(squares * inner_scale + epsilon)
    vectors_list = [start / length[:, None]]
    hessenberg = jnp.zeros((vectors, ITERS + 1, ITERS), jnp.float32)
    for column in range(ITERS):
        operator_vector = vectors_list[column]
        operator_partner = swapped(operator_vector, "side", 0)
        port_part = jnp.where(is_port, operator_vector, operator_partner)
        star_part = jnp.where(is_port, operator_partner, operator_vector)
        parity = jnp.where(is_port, 1.0, -1.0).astype(jnp.float32)
        mirrored_shaped = star_part.reshape(star_part.shape[:-1] + (BLK_DEV, BLOCK))
        field = port_part + parity * jnp.einsum(
            "bij,...bj->...bi", mirror_onehot, mirrored_shaped, precision=lax.Precision.HIGHEST
        ).reshape(star_part.shape)
        near_rounded = field.astype(jnp.bfloat16)
        below_list = []
        above_list = []
        for distance in range(1, WIN + 1):
            below_list.append(shifted(near_rounded, ("grp", "dev"), distance))
            above_list.append(shifted(near_rounded, ("grp", "dev"), -distance))
        window = jnp.concatenate(below_list[::-1] + [near_rounded] + above_list, axis=1)
        picked = window.reshape(vectors, -1, BLOCK)[:, window_cols]
        products = jnp.einsum("rkj,kij->rki", picked, blocks, preferred_element_type=jnp.float32)
        summed = jnp.einsum("bk,rki->rbi", row_onehot, products, precision=lax.Precision.HIGHEST)
        image = 0.5 * field + summed.reshape(vectors, panels)
        returned = swapped(image, "side", 0)
        symmetric = jnp.where(is_port, image, returned)
        antisym = jnp.where(is_port, returned, image)
        vector = 0.5 * (symmetric - antisym)
        shaped = vector.reshape(vector.shape[:-1] + (BLK_DEV, BLOCK))
        image = jnp.where(
            is_port,
            0.5 * (symmetric + antisym),
            jnp.einsum(
                "bij,...bi->...bj", mirror_onehot, shaped, precision=lax.Precision.HIGHEST
            ).reshape(vector.shape),
        )
        stacked = jnp.stack(vectors_list)
        products_local = jnp.sum(image[None] * stacked, axis=2)
        dot_sums = lax.psum(products_local, ("side", "grp", "dev"))
        coeffs = dot_sums * inner_scale
        remainder = image - jnp.einsum(
            "jr,jrp->rp", coeffs, stacked, precision=lax.Precision.HIGHEST
        )
        rem_squares = (
            lax.psum(jnp.sum(remainder * remainder, axis=1), ("side", "grp", "dev")) * inner_scale
        )
        rem_norm = jnp.sqrt(rem_squares + epsilon)
        vectors_list.append(remainder / rem_norm[:, None])
        hessenberg = hessenberg.at[:, : column + 1, column].set(coeffs.T)
        hessenberg = hessenberg.at[:, column + 1, column].set(rem_norm)
    final = jnp.stack(vectors_list)
    return (final[:, None], hessenberg)


def solution(mesh):
    placed = (
        P("side", None, ("grp", "dev")),
        P("side", ("grp", "dev"), None, None),
        P("side", ("grp", "dev")),
        P("side", ("grp", "dev")),
        P(("grp", "dev")),
    )
    return jax.shard_map(
        on_device,
        mesh=mesh,
        in_specs=placed,
        out_specs=(P(None, "side", None, ("grp", "dev")), P()),
        check_vma=False,
    )
```

profile of v0, /device:TPU:1, one launch (start us, length us, event | category | flops | bytes accessed | tf_op | source)
XLA Modules:
  0.0 840.6 jit_solution(13101358596570558061)
XLA Ops:
  0.7 0.9 fusion.35
  1.6 106.1 %psum.49 = f32[8]{0:T(128)S(1)} all-reduce(f32[8]{0:T(128)S(1)} %fusion.35), channel_id=1, replica_groups=mesh['side'=2,'grp'=8,'dev'=32] {'side','grp','dev'}, use_global_device_ids=true, to_apply=%region_1.0 | all-reduce | flops 8 | bytes 64 | tf_op jit(solution)/shard_map/psum | solution.py:45
  107.8 4.7 collective-permute-start
  112.5 0.6 copy-done.4
  113.2 2.9 collective-permute-done
  116.3 2.6 collective-permute-start.1
  118.9 5.9 collective-permute-start.2
  124.8 2.4 collective-permute-start.3
  127.3 2.0 collective-permute-start.4
  129.2 2.3 collective-permute-start.5
  131.6 1.3 collective-permute-start.6
  132.9 1.3 collective-permute-start.7
  134.2 1.3 collective-permute-start.8
  136.0 3.5 collective-permute-done.7
  139.5 1.4 collective-permute-done.8
  141.5 0.6 fusion.7
  142.1 0.7 copy-done.2
  143.0 5.2 collective-permute-start.9
  148.1 3.1 collective-permute-done.9
  151.6 104.0 %psum.50 = f32[1,8]{1,0:T(1,128)S(1)} all-reduce(f32[1,8]{1,0:T(1,128)S(1)} %bitcast.209), channel_id=1, replica_groups=mesh['side'=2,'grp'=8,'dev'=32] {'side','grp','dev'}, use_global_device_ids=true, to_apply=%region_3.4 | all-reduce | flops 8 | bytes 64 | tf_op jit(solution)/shard_map/psum | solution.py:84
  255.9 94.4 %psum.51 = f32[8]{0:T(128)S(1)} all-reduce(f32[8]{0:T(128)S(1)} %get-tuple-element.76), channel_id=1, replica_groups=mesh['side'=2,'grp'=8,'dev'=32] {'side','grp','dev'}, use_global_device_ids=true, to_apply=%region_5.6 | all-reduce | flops 8 | bytes 64 | tf_op jit(solution)/shard_map/psum | solution.py:90
  350.3 4.0 collective-permute-start.10
  354.4 4.3 collective-permute-done.10
  358.9 1.9 collective-permute-start.11
  360.8 7.8 collective-permute-start.12
  368.6 2.7 collective-permute-start.13
  371.3 1.9 collective-permute-start.14
  373.2 2.4 collective-permute-start.15
  375.6 1.3 collective-permute-start.16
  377.0 1.3 collective-permute-start.17
  378.3 1.3 collective-permute-start.18
  380.0 3.5 collective-permute-done.17
  383.5 1.4 collective-permute-done.18
  384.9 0.6 gather_fusion.1
  385.5 0.6 fusion.5
  386.3 4.1 collective-permute-start.19
  390.4 4.2 collective-permute-done.19
  394.9 103.0 %psum.52 = f32[2,8]{1,0:T(2,128)S(1)} all-reduce(f32[2,8]{1,0:T(2,128)S(1)} %get-tuple-element.81), channel_id=1, replica_groups=mesh['side'=2,'grp'=8,'dev'=32] {'side','grp','dev'}, use_global_device_ids=true, to_apply=%region_7.8 | all-reduce | flops 16 | bytes 128 | tf_op jit(solution)/shard_map/psum | solution.py:84
  498.4 94.2 %psum.53 = f32[8]{0:T(128)S(1)} all-reduce(f32[8]{0:T(128)S(1)} %multiply_reduce_fusion.3), channel_id=1, replica_groups=mesh['side'=2,'grp'=8,'dev'=32] {'side','grp','dev'}, use_global_device_ids=true, to_apply=%region_9.10 | all-reduce | flops 8 | bytes 64 | tf_op jit(solution)/shard_map/psum | solution.py:90
  592.7 4.7 collective-permute-start.20
  598.0 3.0 collective-permute-done.20
  601.2 2.6 collective-permute-start.21
  603.8 7.1 collective-permute-start.22
  610.9 1.5 collective-permute-start.23
  612.4 2.9 collective-permute-start.24
  615.3 1.9 collective-permute-start.25
  617.3 1.3 collective-permute-start.26
  618.6 1.3 collective-permute-start.27
  619.9 1.3 collective-permute-start.28
  621.6 4.0 collective-permute-done.27
  625.6 1.4 collective-permute-done.28
  627.0 0.6 gather_fusion.2
  627.6 0.6 fusion.3
  628.4 4.7 collective-permute-start.29
  633.1 0.6 fusion.86
  633.7 0.7 and_reduce_fusion
  634.4 1.3 scatter.24
  635.8 1.0 collective-permute-done.29
  637.1 104.3 %psum.54 = f32[3,8]{1,0:T(4,128)S(1)} all-reduce(f32[3,8]{1,0:T(4,128)S(1)} %get-tuple-element.79), channel_id=1, replica_groups=mesh['side'=2,'grp'=8,'dev'=32] {'side','grp','dev'}, use_global_device_ids=true, to_apply=%region_11.12 | all-reduce | flops 24 | bytes 192 | tf_op jit(solution)/shard_map/psum | solution.py:84
  741.8 94.4 %psum.55 = f32[8]{0:T(128)S(1)} all-reduce(f32[8]{0:T(128)S(1)} %multiply_reduce_fusion.2), channel_id=1, replica_groups=mesh['side'=2,'grp'=8,'dev'=32] {'side','grp','dev'}, use_global_device_ids=true, to_apply=%region_13.14 | all-reduce | flops 8 | bytes 64 | tf_op jit(solution)/shard_map/psum | solution.py:90
  836.3 0.6 maximum_bitcast_fusion
  836.9 1.8 broadcast_select_fusion
  838.7 1.3 scatter.26
  840.0 0.6 copy.9
  (95 shorter events, 6.1 us)
Async XLA Ops:
  0.6 140.8 %copy-start = (bf16[1,32,128,128]{3,2,1,0:T(8,128)(2,1)S(1)}, bf16[1,32,128,128]{3,2,1,0:T(8,128)(2,1)}, u32[]{:S(2)}) copy-start(bf16[1,32,128,128]{3,2,1,0:T(8,128)(2,1)} %param.18) | copy-start | bytes 3145732
  0.6 107.1 %copy-start.1 = (f32[1,8,256]{2,1,0:T(8,128)S(1)}, f32[1,8,256]{2,1,0:T(8,128)}, u32[]{:S(2)}) copy-start(f32[1,8,256]{2,1,0:T(8,128)} %param.17) | copy-start | bytes 24580
  107.8 8.3 collective-permute-start
  112.5 0.7 copy-start.4
  113.2 2.9 copy-start.3
  116.3 15.2 %collective-permute-start.1 = (bf16[8,256]{1,0:T(8,128)(2,1)S(1)}, bf16[8,256]{1,0:T(8,128)(2,1)S(1)}, u32[]{:S(2)}, u32[]{:S(2)}) collective-permute-start(bf16[8,256]{1,0:T(8,128)(2,1)S(1)} %get-tuple-element.98), channel_id=1, source_target_pairs={{0,4},{1,5},{2,6},{3,7},{4,8},{5,9},{6,10},{7,11},{8,12},{9,13},{1... | collective-permute-start | bytes 12296 | tf_op jit(solution)/shard_map/ppermute | solution.py:18
  118.9 14.0 %collective-permute-start.2 = (bf16[8,256]{1,0:T(8,128)(2,1)S(1)}, bf16[8,256]{1,0:T(8,128)(2,1)S(1)}, u32[]{:S(2)}, u32[]{:S(2)}) collective-permute-start(bf16[8,256]{1,0:T(8,128)(2,1)S(1)} %get-tuple-element.98), channel_id=1, source_target_pairs={{0,3},{1,4},{2,5},{3,6},{4,7},{5,8},{6,9},{7,10},{8,11},{9,12},{10... | collective-permute-start | bytes 12296 | tf_op jit(solution)/shard_map/ppermute | solution.py:18
  124.8 9.4 %collective-permute-start.3 = (bf16[8,256]{1,0:T(8,128)(2,1)S(1)}, bf16[8,256]{1,0:T(8,128)(2,1)S(1)}, u32[]{:S(2)}, u32[]{:S(2)}) collective-permute-start(bf16[8,256]{1,0:T(8,128)(2,1)S(1)} %get-tuple-element.98), channel_id=1, source_target_pairs={{0,2},{1,3},{2,4},{3,5},{4,6},{5,7},{6,8},{7,9},{8,10},{9,11},{10,... | collective-permute-start | bytes 12296 | tf_op jit(solution)/shard_map/ppermute | solution.py:18
  127.3 8.3 collective-permute-start.4
  129.2 6.4 collective-permute-start.5
  131.6 4.4 collective-permute-start.6
  132.9 6.6 collective-permute-start.7
  134.2 6.6 collective-permute-start.8
  142.1 0.7 copy-start.2
  143.0 8.3 collective-permute-start.9
  350.3 8.3 collective-permute-start.10
  358.9 16.7 %collective-permute-start.11 = (bf16[8,256]{1,0:T(8,128)(2,1)S(1)}, bf16[8,256]{1,0:T(8,128)(2,1)S(1)}, u32[]{:S(2)}, u32[]{:S(2)}) collective-permute-start(bf16[8,256]{1,0:T(8,128)(2,1)S(1)} %get-tuple-element.102), channel_id=1, source_target_pairs={{0,4},{1,5},{2,6},{3,7},{4,8},{5,9},{6,10},{7,11},{8,12},{9,13},{1... | collective-permute-start | bytes 12296 | tf_op jit(solution)/shard_map/ppermute | solution.py:18
  360.8 16.2 %collective-permute-start.12 = (bf16[8,256]{1,0:T(8,128)(2,1)S(1)}, bf16[8,256]{1,0:T(8,128)(2,1)S(1)}, u32[]{:S(2)}, u32[]{:S(2)}) collective-permute-start(bf16[8,256]{1,0:T(8,128)(2,1)S(1)} %get-tuple-element.102), channel_id=1, source_target_pairs={{0,3},{1,4},{2,5},{3,6},{4,7},{5,8},{6,9},{7,10},{8,11},{9,12},{10... | collective-permute-start | bytes 12296 | tf_op jit(solution)/shard_map/ppermute | solution.py:18
  368.6 9.7 %collective-permute-start.13 = (bf16[8,256]{1,0:T(8,128)(2,1)S(1)}, bf16[8,256]{1,0:T(8,128)(2,1)S(1)}, u32[]{:S(2)}, u32[]{:S(2)}) collective-permute-start(bf16[8,256]{1,0:T(8,128)(2,1)S(1)} %get-tuple-element.102), channel_id=1, source_target_pairs={{0,2},{1,3},{2,4},{3,5},{4,6},{5,7},{6,8},{7,9},{8,10},{9,11},{10,... | collective-permute-start | bytes 12296 | tf_op jit(solution)/shard_map/ppermute | solution.py:18
  371.3 8.3 collective-permute-start.14
  373.2 6.4 collective-permute-start.15
  375.6 4.4 collective-permute-start.16
  377.0 6.5 collective-permute-start.17
  378.3 6.6 collective-permute-start.18
  386.3 8.3 collective-permute-start.19
  592.7 8.3 collective-permute-start.20
  601.2 16.1 %collective-permute-start.21 = (bf16[8,256]{1,0:T(8,128)(2,1)S(1)}, bf16[8,256]{1,0:T(8,128)(2,1)S(1)}, u32[]{:S(2)}, u32[]{:S(2)}) collective-permute-start(bf16[8,256]{1,0:T(8,128)(2,1)S(1)} %get-tuple-element.104), channel_id=1, source_target_pairs={{0,4},{1,5},{2,6},{3,7},{4,8},{5,9},{6,10},{7,11},{8,12},{9,13},{1... | collective-permute-start | bytes 12296 | tf_op jit(solution)/shard_map/ppermute | solution.py:18
  603.8 14.8 %collective-permute-start.22 = (bf16[8,256]{1,0:T(8,128)(2,1)S(1)}, bf16[8,256]{1,0:T(8,128)(2,1)S(1)}, u32[]{:S(2)}, u32[]{:S(2)}) collective-permute-start(bf16[8,256]{1,0:T(8,128)(2,1)S(1)} %get-tuple-element.104), channel_id=1, source_target_pairs={{0,3},{1,4},{2,5},{3,6},{4,7},{5,8},{6,9},{7,10},{8,11},{9,12},{10... | collective-permute-start | bytes 12296 | tf_op jit(solution)/shard_map/ppermute | solution.py:18
  610.9 9.0 %collective-permute-start.23 = (bf16[8,256]{1,0:T(8,128)(2,1)S(1)}, bf16[8,256]{1,0:T(8,128)(2,1)S(1)}, u32[]{:S(2)}, u32[]{:S(2)}) collective-permute-start(bf16[8,256]{1,0:T(8,128)(2,1)S(1)} %get-tuple-element.104), channel_id=1, source_target_pairs={{0,2},{1,3},{2,4},{3,5},{4,6},{5,7},{6,8},{7,9},{8,10},{9,11},{10,... | collective-permute-start | bytes 12296 | tf_op jit(solution)/shard_map/ppermute | solution.py:18
  612.4 8.8 %collective-permute-start.24 = (bf16[8,256]{1,0:T(8,128)(2,1)S(1)}, bf16[8,256]{1,0:T(8,128)(2,1)S(1)}, u32[]{:S(2)}, u32[]{:S(2)}) collective-permute-start(bf16[8,256]{1,0:T(8,128)(2,1)S(1)} %get-tuple-element.104), channel_id=1, source_target_pairs={{0,1},{1,2},{2,3},{3,4},{4,5},{5,6},{6,7},{7,8},{8,9},{9,10},{10,1... | collective-permute-start | bytes 12296 | tf_op jit(solution)/shard_map/ppermute | solution.py:18
  615.3 5.9 collective-permute-start.25
  617.3 4.4 collective-permute-start.26
  618.6 7.0 collective-permute-start.27
  619.9 7.1 collective-permute-start.28
  628.4 8.3 collective-permute-start.29
where the time goes:
time: 842 us; the launch traced here: 841 us
  blocking collectives  700 us (83%)
  starting transfers between devices  86.9 us (10%)
  waiting for transfers between devices  34.7 us (4%)
    psum x3, blocking collectives, on_device(): dot_sums = lax.psum(products_local, ('side', 'grp', 'dev'))  311 us
    psum x3, blocking collectives, on_device(): lax.psum(jnp.sum(remainder * remainder, axis=1), ('side', 'grp', 'dev'))  283 us
    psum x1, blocking collectives, on_device(): squares = lax.psum(jnp.sum(start * start, axis=1), ('side', 'grp', 'dev'))  106 us
    ppermute x24, starting transfers between devices, shifted(): return lax.ppermute(block, axis, route)  59.5 us
    ppermute x6, starting transfers between devices, swapped(): lax.ppermute(value, axis, [(i, i ^ 1 << distance) for i in range(lax.axis...  27.3 us
    ppermute x6, waiting for transfers between devices, swapped(): lax.ppermute(value, axis, [(i, i ^ 1 << distance) for i in range(lax.axis...  18.5 us
  transfers between devices with their start and end apart: 30, of which 15 were waited for; matrix products, arithmetic and copies ran while one was open for 0% of the time, Pallas kernels for 0%

commit v1 on v0

v1 whole, which is shorter than its diff:
```python
import jax
import jax.numpy as jnp
from jax import lax
from jax.experimental import pallas as pl
from jax.experimental.pallas import tpu as pltpu
from jax.sharding import PartitionSpec as P

BLOCK = 128
BLK_DEV = 2
WIN = 4
ITERS = 3
NB_DEV = 32
NRHS = 8
N_GRP = 8
N_DEV = 32
TOTAL_PANELS = 131072.0
EPSILON = 1e-06
OWN = WIN * BLK_DEV
MESH = pl.DeviceIdType.MESH
PAIRS = [(i, j) for j in range(ITERS + 1) for i in range(j + 1)]


def lane_gather(x, index):
    return jnp.take_along_axis(x, index, axis=1, mode="promise_in_bounds")


def coefficients(gram):
    def dot(a, b):
        total = None
        for i, ai in enumerate(a):
            row = None
            for j, bj in enumerate(b):
                term = gram[(min(i, j), max(i, j))] * bj
                row = term if row is None else row + term
            total = ai * row if total is None else total + ai * row
        return total

    c = [[1.0 / jnp.sqrt(gram[(0, 0)] + EPSILON)]]
    h = {}
    for k in range(ITERS):
        w = [0.5 * v for v in c[k]] + [c[k][k]]
        for i in range(1, k + 1):
            w[i] = w[i] + c[k][i - 1]
        u = list(w)
        for j in range(k + 1):
            h[(j, k)] = dot(w, c[j])
            for i in range(j + 1):
                u[i] = u[i] - h[(j, k)] * c[j][i]
        norm = jnp.sqrt(jnp.maximum(dot(u, u), 0.0) + EPSILON)
        h[(k + 1, k)] = norm
        c.append([v / norm for v in u])
    return c, h


def kernel(
    x_ref, nb_hbm, rows_ref, cols_ref, mirror_ref, q_ref, h_ref,
    nb, win0, win1, win2, xs, xr, z3, zr, red,
    nb_sem, swap_send, swap_recv, halo_send, halo_recv, zx_send, zx_recv, red_send, red_recv,
):
    side = lax.axis_index("side")
    grp = lax.axis_index("grp")
    dev = lax.axis_index("dev")
    owner = grp * N_DEV + dev
    is_port = side == 0
    chip_x, y_lo, core = dev // 8, (dev // 2) % 4, dev % 2
    in_a = chip_x * 2 + core
    in_b = side * 4 + y_lo

    load = pltpu.make_async_copy(nb_hbm.at[0], nb, nb_sem)
    load.start()

    partner = (1 - side, grp, dev)

    def halo_device(distance):
        other = (owner + distance + N_GRP * N_DEV) % (N_GRP * N_DEV)
        return (side, other // N_DEV, other % N_DEV)

    def member(stage, flip):
        if stage == 0:
            other = in_a ^ flip
            return (side, grp, (other // 2) * 8 + y_lo * 2 + other % 2)
        if stage == 1:
            other = in_b ^ flip
            return (other // 4, grp, chip_x * 8 + (other % 4) * 2 + core)
        return (side, grp ^ flip, dev)

    slot = (in_a, in_b, grp)
    distances = [d for d in range(-WIN, WIN + 1) if d]

    barrier = pltpu.get_barrier_semaphore()
    met = [halo_device(d) for d in distances]
    met += [member(s, f) for s in range(3) for f in range(1, 8)]
    for device in met:
        pl.semaphore_signal(barrier, inc=1, device_id=device, device_id_type=MESH)

    index = [
        jnp.broadcast_to(mirror_ref[b : b + 1, :], (NRHS, BLOCK)) for b in range(BLK_DEV)
    ]
    own = [x_ref[0, :, b * BLOCK : (b + 1) * BLOCK] for b in range(BLK_DEV)]
    star = [lane_gather(own[b], index[b]) for b in range(BLK_DEV)]
    for b in range(BLK_DEV):
        xs[b] = jnp.where(is_port, own[b], star[b])

    pl.semaphore_wait(barrier, len(met))

    swap = pltpu.make_async_remote_copy(
        src_ref=xs, dst_ref=xr, send_sem=swap_send, recv_sem=swap_recv,
        device_id=partner, device_id_type=MESH,
    )
    swap.start()

    inverse = []
    for b in range(BLK_DEV):
        where_to = lax.broadcasted_iota(jnp.int32, (BLOCK, BLOCK), 0)
        onehot = jnp.where(
            jnp.broadcast_to(mirror_ref[b : b + 1, :], (BLOCK, BLOCK)) == where_to, 1.0, 0.0
        ).astype(jnp.bfloat16)
        lanes = lax.broadcasted_iota(jnp.int32, (16, BLOCK), 1).astype(jnp.float32).astype(jnp.bfloat16)
        found = lax.dot_general(
            lanes, onehot, (((1,), (1,)), ((), ())), preferred_element_type=jnp.float32
        )
        inverse.append(found[:NRHS].astype(jnp.int32))

    swap.wait_recv()
    z = [[None] * BLK_DEV for _ in range(ITERS + 1)]
    for b in range(BLK_DEV):
        other = xr[b]
        z[0][b] = jnp.where(is_port, own[b] + other, other - star[b])

    copies = [swap]
    exchanged = []
    load.wait()
    for k, win in enumerate((win0, win1, win2)):
        for b in range(BLK_DEV):
            win[OWN + b] = z[k][b].astype(jnp.bfloat16)
        hops = []
        for n, d in enumerate(distances):
            copy = pltpu.make_async_remote_copy(
                src_ref=win.at[pl.ds(OWN, BLK_DEV)],
                dst_ref=win.at[pl.ds((WIN - d) * BLK_DEV, BLK_DEV)],
                send_sem=halo_send.at[k, n],
                recv_sem=halo_recv.at[k, n],
                device_id=halo_device(d),
                device_id_type=MESH,
            )
            copy.start()
            hops.append(copy)
        copies += hops
        for copy in hops:
            copy.wait_recv()
        total = jnp.zeros((16, BLOCK), jnp.float32)
        for e in range(0, NB_DEV, 2):
            lefts, rights = [], []
            for f in (e, e + 1):
                place = cols_ref[0, f] - (owner - WIN) * BLK_DEV
                place = jnp.clip(place, 0, (2 * WIN + 1) * BLK_DEV - 1)
                picked = win[place].astype(jnp.float32)
                low = (rows_ref[0, f] == 0).astype(jnp.float32)
                lefts.append(
                    jnp.concatenate([picked * low, picked * (1.0 - low)], axis=0).astype(jnp.bfloat16)
                )
                rights.append(nb[f])
            total = total + lax.dot_general(
                jnp.concatenate(lefts, axis=1),
                jnp.concatenate(rights, axis=1),
                (((1,), (1,)), ((), ())),
                preferred_element_type=jnp.float32,
            )
        z[k + 1] = [total[:NRHS], total[NRHS:]]
        for b in range(BLK_DEV):
            z3[k, b] = z[k + 1][b]
        if k < ITERS:
            copy = pltpu.make_async_remote_copy(
                src_ref=z3.at[k], dst_ref=zr.at[k],
                send_sem=zx_send.at[k], recv_sem=zx_recv.at[k],
                device_id=partner, device_id_type=MESH,
            )
            copy.start()
            copies.append(copy)
            exchanged.append(copy)

    lane = lax.broadcasted_iota(jnp.int32, (NRHS, BLOCK), 1)
    partial = jnp.zeros((NRHS, BLOCK), jnp.float32)
    for p, (i, j) in enumerate(PAIRS):
        product = z[i][0] * z[j][0] + z[i][1] * z[j][1]
        partial = jnp.where(lane == p, jnp.sum(product, axis=1, keepdims=True), partial)

    for stage in range(3):
        red[stage, slot[stage]] = partial
        hops = []
        for flip in range(1, 8):
            copy = pltpu.make_async_remote_copy(
                src_ref=red.at[stage, slot[stage]],
                dst_ref=red.at[stage, slot[stage]],
                send_sem=red_send.at[stage, flip],
                recv_sem=red_recv.at[stage, flip],
                device_id=member(stage, flip),
                device_id_type=MESH,
            )
            copy.start()
            hops.append(copy)
        copies += hops
        if stage == 0:
            images = [own]
            for k in range(ITERS):
                exchanged[k].wait_recv()
                image = []
                for b in range(BLK_DEV):
                    mine, other = z[k + 1][b], zr[k, b]
                    port = 0.5 * (mine + other)
                    starboard = lane_gather(0.5 * (other - mine), inverse[b])
                    image.append(jnp.where(is_port, port, starboard))
                images.append(image)
        for copy in hops:
            copy.wait_recv()
        partial = red[stage, 0]
        for n in range(1, 8):
            partial = partial + red[stage, n]

    scaled = partial * (0.5 / TOTAL_PANELS)
    gram = {
        pair: jnp.broadcast_to(scaled[:, p : p + 1], (NRHS, BLOCK)) for p, pair in enumerate(PAIRS)
    }
    c, h = coefficients(gram)
    for j in range(ITERS + 1):
        for b in range(BLK_DEV):
            value = c[j][0] * images[0][b]
            for i in range(1, j + 1):
                value = value + c[j][i] * images[i][b]
            q_ref[j, 0, :, b * BLOCK : (b + 1) * BLOCK] = value
    table = jnp.zeros((NRHS, BLOCK), jnp.float32)
    for (j, k), value in h.items():
        table = jnp.where(lane == k * (ITERS + 1) + j, value, table)
    turned = jnp.transpose(table)
    for k in range(ITERS):
        h_ref[k] = turned[k * (ITERS + 1) : (k + 1) * (ITERS + 1), :]
    for copy in copies:
        copy.wait_send()


def on_device(sources, near_blocks, block_rows, block_cols, mirror):
    vmem = pl.BlockSpec(memory_space=pltpu.VMEM)
    smem = pl.BlockSpec(memory_space=pltpu.SMEM)
    f32, bf16 = jnp.float32, jnp.bfloat16
    dma = pltpu.SemaphoreType.DMA
    q, h = pl.pallas_call(
        kernel,
        out_shape=(
            jax.ShapeDtypeStruct((ITERS + 1, 1, NRHS, BLK_DEV * BLOCK), f32),
            jax.ShapeDtypeStruct((ITERS, ITERS + 1, NRHS), f32),
        ),
        in_specs=[vmem, pl.BlockSpec(memory_space=pl.ANY), smem, smem, vmem],
        out_specs=(vmem, vmem),
        scratch_shapes=[
            pltpu.VMEM((NB_DEV, BLOCK, BLOCK), bf16),
            *[pltpu.VMEM(((2 * WIN + 1) * BLK_DEV, NRHS, BLOCK), bf16)] * ITERS,
            pltpu.VMEM((BLK_DEV, NRHS, BLOCK), f32),
            pltpu.VMEM((BLK_DEV, NRHS, BLOCK), f32),
            pltpu.VMEM((ITERS, BLK_DEV, NRHS, BLOCK), f32),
            pltpu.VMEM((ITERS, BLK_DEV, NRHS, BLOCK), f32),
            pltpu.VMEM((3, 8, NRHS, BLOCK), f32),
            dma,
            dma, dma,
            dma((ITERS, 2 * WIN)), dma((ITERS, 2 * WIN)),
            dma((ITERS,)), dma((ITERS,)),
            dma((3, 8)), dma((3, 8)),
        ],
        compiler_params=pltpu.CompilerParams(
            collective_id=0, has_side_effects=True, vmem_limit_bytes=8 * 1024 * 1024
        ),
    )(sources, near_blocks, block_rows, block_cols, mirror.reshape(BLK_DEV, BLOCK))
    return q, jnp.transpose(h)


def solution(mesh):
    placed = (
        P("side", None, ("grp", "dev")),
        P("side", ("grp", "dev"), None, None),
        P("side", ("grp", "dev")),
        P("side", ("grp", "dev")),
        P(("grp", "dev")),
    )
    return jax.shard_map(
        on_device,
        mesh=mesh,
        in_specs=placed,
        out_specs=(P(None, "side", None, ("grp", "dev")), P()),
        check_vma=False,
    )
```

time: 842 us -> 58.7 us (0.07)
  blocking collectives: 700 us -> 0 us
  starting transfers between devices: 86.9 us -> 0 us
  Pallas kernels: 0 us -> 52.8 us
  waiting for transfers between devices: 34.7 us -> 0 us
    psum x7 -> x0, blocking collectives: 700 us -> none  [the longest x3 311 us: on_device(): dot_sums = lax.psum(products_local, ('side', 'grp', 'dev'))]
    ppermute x30 -> x0, starting transfers between devices: 86.9 us -> none  [the longest x24 59.5 us: shifted(): return lax.ppermute(block, axis, route)]
    pallas_call x0 -> x1, Pallas kernels: none -> 52.8 us  [on_device(): pl.pallas_call(kernel, out_shape=(jax.ShapeDtypeStruct((ITERS + 1, 1, NRH...]
    ppermute x30 -> x0, waiting for transfers between devices: 34.7 us -> none  [the longest x6 18.5 us: swapped(): lax.ppermute(value, axis, [(i, i ^ 1 << distance) for i in range(lax.axis...]
  transfers between devices with their start and end apart: 30 -> 0, of which waited for: 15 -> 0; matrix products, arithmetic and copies ran while one was open for 0% -> 0% of each run, Pallas kernels for 0% -> 0%
where the time goes in v1:
time: 58.7 us; the launch traced here: 57.9 us
  Pallas kernels  52.8 us (90%)
  local copies, waits for them, and re-layouts  4.45 us (8%)
  between operations  0.66 us (1%)
    pallas_call x1, Pallas kernels, on_device(): pl.pallas_call(kernel, out_shape=(jax.ShapeDtypeStruct((ITERS + 1, 1, NRH...  52.8 us
    unnamed x12, local copies, waits for them, and re-layouts  4.45 us

profile of v1, /device:TPU:1, one launch (start us, length us, event | category | flops | bytes accessed | tf_op | source)
XLA Modules:
  0.0 57.9 jit_solution(6776097852850368345)
XLA Ops:
  0.6 0.0 copy-start.2
  0.6 0.0 copy-start.3
  0.7 0.7 %copy-done.2 = s32[256]{0:T(256)S(1)} copy-done((s32[256]{0:T(256)S(1)}, s32[256]{0:T(256)}, u32[]{:S(2)}) %copy-start.2) | copy-done | bytes 1048
  1.3 0.0 copy-done.3
  1.3 0.0 copy-start
  1.3 1.2 %copy-done = bf16[1,32,128,128]{3,2,1,0:T(8,128)(2,1)S(1)} copy-done((bf16[1,32,128,128]{3,2,1,0:T(8,128)(2,1)S(1)}, bf16[1,32,128,128]{3,2,1,0:T(8,128)(2,1)}, u32[]{:S(2)}) %copy-start) | copy-done | bytes 1048600
  2.5 0.0 copy-start.1
  2.5 0.7 %copy-done.1 = f32[1,8,256]{2,1,0:T(8,128)S(1)} copy-done((f32[1,8,256]{2,1,0:T(8,128)S(1)}, f32[1,8,256]{2,1,0:T(8,128)}, u32[]{:S(2)}) %copy-start.1) | copy-done | bytes 8216
  3.2 0.0 copy-start.4
  3.2 0.7 %copy-done.4 = s32[1,32]{1,0:T(1,128)S(1)} copy-done((s32[1,32]{1,0:T(1,128)S(1)}, s32[1,32]{1,0:T(1,128)}, u32[]{:S(2)}) %copy-start.4) | copy-done | bytes 152
  3.9 52.8 %shard_map.68 = (f32[4,1,8,256]{3,2,1,0:T(8,128)S(1)}, f32[3,4,8]{2,1,0:T(4,128)S(1)}) custom-call(f32[1,8,256]{2,1,0:T(8,128)S(1)} %copy-done.1, bf16[1,32,128,128]{3,2,1,0:T(8,128)(2,1)S(1)} %copy-done, s32[1,32]{1,0:T(1,128)S(1)} %copy-done.3, s32[1,32]{1,0:T(1,128)S(1)} %copy-done.4, s32[2,128]{1,0:T(2,128)S(1)} %bitcast.3), custom_call_target="tpu_custom_call" | custom-call | tf_op jit(solution)/shard_map/pallas_call | solution.py:246
  56.7 0.6 %copy.9 = f32[4,1,8,256]{3,2,1,0:T(8,128)} copy(f32[4,1,8,256]{3,2,1,0:T(8,128)S(1)} %get-tuple-element.8) | data formatting | bytes 65536
  57.3 0.6 %copy.10 = f32[8,4,3]{0,1,2:T(4,128)} copy(f32[8,4,3]{0,1,2:T(4,128)S(1)} %bitcast.2) | data formatting | bytes 768
Async XLA Ops:
  0.6 0.7 %copy-start.2 = (s32[256]{0:T(256)S(1)}, s32[256]{0:T(256)}, u32[]{:S(2)}) copy-start(s32[256]{0:T(256)} %param.9) | copy-start | bytes 3076
  0.6 0.7 %copy-start.3 = (s32[1,32]{1,0:T(1,128)S(1)}, s32[1,32]{1,0:T(1,128)}, u32[]{:S(2)}) copy-start(s32[1,32]{1,0:T(1,128)} %rows_ref.1) | copy-start | bytes 388
  1.3 1.2 %copy-start = (bf16[1,32,128,128]{3,2,1,0:T(8,128)(2,1)S(1)}, bf16[1,32,128,128]{3,2,1,0:T(8,128)(2,1)}, u32[]{:S(2)}) copy-start(bf16[1,32,128,128]{3,2,1,0:T(8,128)(2,1)} %nb_hbm.1) | copy-start | bytes 3145732
  2.5 0.7 %copy-start.1 = (f32[1,8,256]{2,1,0:T(8,128)S(1)}, f32[1,8,256]{2,1,0:T(8,128)}, u32[]{:S(2)}) copy-start(f32[1,8,256]{2,1,0:T(8,128)} %x_ref.1) | copy-start | bytes 24580
  3.2 0.7 %copy-start.4 = (s32[1,32]{1,0:T(1,128)S(1)}, s32[1,32]{1,0:T(1,128)}, u32[]{:S(2)}) copy-start(s32[1,32]{1,0:T(1,128)} %cols_ref.1) | copy-start | bytes 388

commit v2 on v1

v2 whole, which is shorter than its diff:
```python
import jax
import jax.numpy as jnp
from jax import lax
from jax.experimental import pallas as pl
from jax.experimental.pallas import tpu as pltpu
from jax.sharding import PartitionSpec as P

BLOCK = 128
BLK_DEV = 2
WIN = 4
ITERS = 3
NB_DEV = 32
NRHS = 8
N_GRP = 8
N_DEV = 32
TOTAL_PANELS = 131072.0
EPSILON = 1e-06
SLOTS = (2 * WIN + 1) * BLK_DEV
OWN = WIN * BLK_DEV
MESH = pl.DeviceIdType.MESH
PAIRS = [(i, j) for j in range(ITERS + 1) for i in range(j + 1)]
STAGE_SIZES = (16, 32)
DISTANCES = [4, -4, 3, -3, 2, -2, 1, -1]


def lane_gather(x, index):
    return jnp.take_along_axis(x, index, axis=1, mode="promise_in_bounds")


def coefficients(gram):
    def dot(a, b):
        total = None
        for i, ai in enumerate(a):
            row = None
            for j, bj in enumerate(b):
                term = gram[(min(i, j), max(i, j))] * bj
                row = term if row is None else row + term
            total = ai * row if total is None else total + ai * row
        return total

    c = [[1.0 / jnp.sqrt(gram[(0, 0)] + EPSILON)]]
    h = {}
    for k in range(ITERS):
        w = [0.5 * v for v in c[k]] + [c[k][k]]
        for i in range(1, k + 1):
            w[i] = w[i] + c[k][i - 1]
        u = list(w)
        for j in range(k + 1):
            h[(j, k)] = dot(w, c[j])
            for i in range(j + 1):
                u[i] = u[i] - h[(j, k)] * c[j][i]
        norm = jnp.sqrt(jnp.maximum(dot(u, u), 0.0) + EPSILON)
        h[(k + 1, k)] = norm
        c.append([v / norm for v in u])
    return c, h


def kernel(
    x_hbm, nb_hbm, rows_hbm, cols_hbm, mirror_hbm, q_ref, h_ref,
    x_ref, nb, rows_ref, cols_ref, mirror_ref,
    wina, winb, win1, win2, xs, xr, zs, zr, red0, red1,
    load_sem, swap_send, swap_recv, cross_send, cross_recv, halo_send, halo_recv,
    zx_send, zx_recv, red_send, red_recv,
):
    side = lax.axis_index("side")
    grp = lax.axis_index("grp")
    dev = lax.axis_index("dev")
    owner = grp * N_DEV + dev
    is_port = side == 0
    chip_x, y_lo, core = dev // 8, (dev // 2) % 4, dev % 2
    place = (grp * 2 + core, chip_x * 8 + side * 4 + y_lo)

    def near(distance, across):
        other = (owner + distance + N_GRP * N_DEV) % (N_GRP * N_DEV)
        return (1 - side if across else side, other // N_DEV, other % N_DEV)

    def member(stage, flip):
        other = place[stage] ^ flip
        if stage == 0:
            return (side, other // 2, chip_x * 8 + y_lo * 2 + other % 2)
        return ((other // 4) % 2, grp, (other // 8) * 8 + (other % 4) * 2 + core)

    barrier = pltpu.get_barrier_semaphore()
    met = [near(d, across) for d in DISTANCES for across in (False, True)]
    met += [member(s, f) for s in (1, 0) for f in range(1, STAGE_SIZES[s])]
    for device in met:
        pl.semaphore_signal(barrier, inc=1, device_id=device, device_id_type=MESH)

    loads = [
        pltpu.make_async_copy(source, target, load_sem.at[n])
        for n, (source, target) in enumerate(
            (
                (x_hbm, x_ref),
                (mirror_hbm, mirror_ref),
                (cols_hbm, cols_ref),
                (rows_hbm, rows_ref),
                (nb_hbm.at[0], nb),
            )
        )
    ]
    for load in loads:
        load.start()
    loads[0].wait()
    loads[1].wait()

    index = [
        jnp.broadcast_to(mirror_ref[b : b + 1, :], (NRHS, BLOCK)) for b in range(BLK_DEV)
    ]
    own = [x_ref[0, :, b * BLOCK : (b + 1) * BLOCK] for b in range(BLK_DEV)]
    star = [lane_gather(own[b], index[b]) for b in range(BLK_DEV)]
    for b in range(BLK_DEV):
        sent = jnp.where(is_port, own[b], star[b])
        xs[b] = sent
        wina[OWN + b] = sent.astype(jnp.bfloat16)

    pl.semaphore_wait(barrier, len(met))

    copies = []

    def send(source, target, send_sem, recv_sem, device):
        copy = pltpu.make_async_remote_copy(
            src_ref=source, dst_ref=target, send_sem=send_sem, recv_sem=recv_sem,
            device_id=device, device_id_type=MESH,
        )
        copy.start()
        copies.append(copy)
        return copy

    partner = (1 - side, grp, dev)
    swap = send(xs, xr, swap_send, swap_recv, partner)

    def halo(k, window, target, across, send_sem, recv_sem, n, d):
        return send(
            window.at[pl.ds(OWN, BLK_DEV)],
            target.at[pl.ds((WIN - d) * BLK_DEV, BLK_DEV)],
            send_sem, recv_sem, near(d, across),
        )

    hops = []
    for n, d in enumerate(DISTANCES):
        hops.append(halo(0, wina, wina, False, halo_send.at[0, n], halo_recv.at[0, n], n, d))
        hops.append(halo(0, wina, winb, True, cross_send.at[n], cross_recv.at[n], n, d))

    inverse = []
    for b in range(BLK_DEV):
        where_to = lax.broadcasted_iota(jnp.int32, (BLOCK, BLOCK), 0)
        onehot = jnp.where(
            jnp.broadcast_to(mirror_ref[b : b + 1, :], (BLOCK, BLOCK)) == where_to, 1.0, 0.0
        ).astype(jnp.bfloat16)
        lanes = lax.broadcasted_iota(jnp.int32, (16, BLOCK), 1).astype(jnp.float32).astype(jnp.bfloat16)
        found = lax.dot_general(
            lanes, onehot, (((1,), (1,)), ((), ())), preferred_element_type=jnp.float32
        )
        inverse.append(found[:NRHS].astype(jnp.int32))

    lane = lax.broadcasted_iota(jnp.int32, (NRHS, BLOCK), 1)
    sublane = lax.broadcasted_iota(jnp.int32, (NRHS, BLOCK), 0)
    sign = jnp.where(is_port, 1.0, -1.0)

    swap.wait_recv()
    z = [[None] * BLK_DEV for _ in range(ITERS + 1)]
    for b in range(BLK_DEV):
        z[0][b] = xr[b] + sign * xs[b]
        winb[OWN + b] = xr[b].astype(jnp.bfloat16)

    for load in loads[2:]:
        load.wait()
    where_from = [
        jnp.clip(cols_ref[0, e] - (owner - WIN) * BLK_DEV, 0, SLOTS - 1) for e in range(NB_DEV)
    ]
    upper = [(rows_ref[0, e] == 0).astype(jnp.float32) for e in range(NB_DEV)]

    def products(windows):
        total = jnp.zeros((16 * len(windows), BLOCK), jnp.float32)
        for e in range(0, NB_DEV, 2):
            lefts, rights = [], []
            for f in (e, e + 1):
                parts = []
                for window in windows:
                    picked = window[where_from[f]].astype(jnp.float32)
                    parts += [picked * upper[f], picked * (1.0 - upper[f])]
                lefts.append(jnp.concatenate(parts, axis=0).astype(jnp.bfloat16))
                rights.append(nb[f])
            total = total + lax.dot_general(
                jnp.concatenate(lefts, axis=1),
                jnp.concatenate(rights, axis=1),
                (((1,), (1,)), ((), ())),
                preferred_element_type=jnp.float32,
            )
        return total

    exchanged = []
    for k in range(ITERS):
        if k > 0:
            window = (None, win1, win2)[k]
            for b in range(BLK_DEV):
                window[OWN + b] = z[k][b].astype(jnp.bfloat16)
            hops = [
                halo(k, window, window, False, halo_send.at[k, n], halo_recv.at[k, n], n, d)
                for n, d in enumerate(DISTANCES)
            ]
            for b in range(BLK_DEV):
                zs[k - 1, b] = z[k][b]
            exchanged.append(
                send(zs.at[k - 1], zr.at[k - 1], zx_send.at[k - 1], zx_recv.at[k - 1], partner)
            )
        for copy in hops:
            copy.wait_recv()
        if k == 0:
            total = products([wina, winb])
            total = sign * total[:16] + total[16:]
        else:
            total = products([window])
        z[k + 1] = [total[:NRHS], total[NRHS:]]

    partial = jnp.zeros((NRHS, BLOCK), jnp.float32)
    for p, (i, j) in enumerate(PAIRS):
        product = z[i][0] * z[j][0] + z[i][1] * z[j][1]
        partial = jnp.where(
            lane == p * NRHS + sublane, jnp.sum(product, axis=1, keepdims=True), partial
        )
    row = jnp.sum(partial, axis=0, keepdims=True)

    for stage, red in enumerate((red0, red1)):
        size = STAGE_SIZES[stage]
        red[place[stage]] = row
        hops = [
            send(
                red.at[place[stage]], red.at[place[stage]],
                red_send.at[stage, flip], red_recv.at[stage, flip], member(stage, flip),
            )
            for flip in range(size - 1, 0, -1)
        ]
        if stage == 0:
            for b in range(BLK_DEV):
                zs[ITERS - 1, b] = z[ITERS][b]
            exchanged.append(
                send(
                    zs.at[ITERS - 1], zr.at[ITERS - 1],
                    zx_send.at[ITERS - 1], zx_recv.at[ITERS - 1], partner,
                )
            )
        if stage == 1:
            images = [own]
            for k in range(ITERS):
                exchanged[k].wait_recv()
                image = []
                for b in range(BLK_DEV):
                    mine, other = z[k + 1][b], zr[k, b]
                    port = 0.5 * (mine + other)
                    starboard = lane_gather(0.5 * (other - mine), inverse[b])
                    image.append(jnp.where(is_port, port, starboard))
                images.append(image)
        for copy in hops:
            copy.wait_recv()
        parts = [red[n] for n in range(size)]
        while len(parts) > 1:
            parts = [a + b for a, b in zip(parts[::2], parts[1::2], strict=True)]
        row = parts[0]

    spread = jnp.broadcast_to(row * (0.5 / TOTAL_PANELS), (NRHS, BLOCK))
    gram = {}
    for p, pair in enumerate(PAIRS):
        chosen = jnp.where(lane == p * NRHS + sublane, spread, 0.0)
        gram[pair] = jnp.broadcast_to(jnp.sum(chosen, axis=1, keepdims=True), (NRHS, BLOCK))
    c, h = coefficients(gram)
    for j in range(ITERS + 1):
        for b in range(BLK_DEV):
            value = c[j][0] * images[0][b]
            for i in range(1, j + 1):
                value = value + c[j][i] * images[i][b]
            q_ref[j, 0, :, b * BLOCK : (b + 1) * BLOCK] = value
    table = jnp.zeros((NRHS, BLOCK), jnp.float32)
    for (j, k), value in h.items():
        table = jnp.where(lane == k * (ITERS + 1) + j, value, table)
    turned = jnp.transpose(table)
    for k in range(ITERS):
        h_ref[k] = turned[k * (ITERS + 1) : (k + 1) * (ITERS + 1), :]
    for copy in copies:
        copy.wait_send()


def on_device(sources, near_blocks, block_rows, block_cols, mirror):
    vmem = pl.BlockSpec(memory_space=pltpu.VMEM)
    hbm = pl.BlockSpec(memory_space=pltpu.HBM)
    f32, bf16 = jnp.float32, jnp.bfloat16
    dma = pltpu.SemaphoreType.DMA
    window = pltpu.VMEM((SLOTS, NRHS, BLOCK), bf16)
    blocks = pltpu.VMEM((BLK_DEV, NRHS, BLOCK), f32)
    steps = pltpu.VMEM((ITERS, BLK_DEV, NRHS, BLOCK), f32)
    q, h = pl.pallas_call(
        kernel,
        out_shape=(
            jax.ShapeDtypeStruct((ITERS + 1, 1, NRHS, BLK_DEV * BLOCK), f32),
            jax.ShapeDtypeStruct((ITERS, ITERS + 1, NRHS), f32),
        ),
        in_specs=[hbm] * 5,
        out_specs=(vmem, vmem),
        scratch_shapes=[
            pltpu.VMEM((1, NRHS, BLK_DEV * BLOCK), f32),
            pltpu.VMEM((NB_DEV, BLOCK, BLOCK), bf16),
            pltpu.SMEM((1, NB_DEV), jnp.int32),
            pltpu.SMEM((1, NB_DEV), jnp.int32),
            pltpu.VMEM((BLK_DEV, BLOCK), jnp.int32),
            window, window, window, window,
            blocks, blocks,
            steps, steps,
            *[pltpu.VMEM((size, 1, BLOCK), f32) for size in STAGE_SIZES],
            dma((5,)),
            dma, dma,
            dma((2 * WIN,)), dma((2 * WIN,)),
            dma((ITERS, 2 * WIN)), dma((ITERS, 2 * WIN)),
            dma((ITERS,)), dma((ITERS,)),
            dma((2, 32)), dma((2, 32)),
        ],
        compiler_params=pltpu.CompilerParams(
            collective_id=0, has_side_effects=True, vmem_limit_bytes=8 * 1024 * 1024
        ),
    )(
        *[
            pltpu.with_memory_space_constraint(operand, pltpu.HBM)
            for operand in (
                sources, near_blocks, block_rows, block_cols, mirror.reshape(BLK_DEV, BLOCK)
            )
        ]
    )
    return q, jnp.transpose(h)


def solution(mesh):
    placed = (
        P("side", None, ("grp", "dev")),
        P("side", ("grp", "dev"), None, None),
        P("side", ("grp", "dev")),
        P("side", ("grp", "dev")),
        P(("grp", "dev")),
    )
    return jax.shard_map(
        on_device,
        mesh=mesh,
        in_specs=placed,
        out_specs=(P(None, "side", None, ("grp", "dev")), P()),
        check_vma=False,
    )
```

time: 58.7 us -> 48.4 us (0.82)
  Pallas kernels: 52.8 us -> 46.4 us
  local copies, waits for them, and re-layouts: 4.45 us -> 1.21 us
    pallas_call x1, Pallas kernels: 52.8 us -> 46.4 us  [on_device(): pl.pallas_call(kernel, out_shape=(jax.ShapeDtypeStruct((ITERS + 1, 1, NRH...]
    unnamed x12 -> x2, local copies, waits for them, and re-layouts: 4.45 us -> 1.21 us
where the time goes in v2:
time: 48.4 us; the launch traced here: 48.2 us
  Pallas kernels  46.4 us (96%)
  local copies, waits for them, and re-layouts  1.21 us (2%)
  between operations  0.64 us (1%)
    pallas_call x1, Pallas kernels, on_device(): pl.pallas_call(kernel, out_shape=(jax.ShapeDtypeStruct((ITERS + 1, 1, NRH...  46.4 us
    unnamed x2, local copies, waits for them, and re-layouts  1.21 us

profile of v2, /device:TPU:1, one launch (start us, length us, event | category | flops | bytes accessed | tf_op | source)
XLA Modules:
  0.0 48.2 jit_solution(13936509087965569492)
XLA Ops:
  0.6 46.4 %shard_map.68 = (f32[4,1,8,256]{3,2,1,0:T(8,128)S(1)}, f32[3,4,8]{2,1,0:T(4,128)S(1)}) custom-call(f32[1,8,256]{2,1,0:T(8,128)} %x_hbm.1, bf16[1,32,128,128]{3,2,1,0:T(8,128)(2,1)} %nb_hbm.1, s32[1,32]{1,0:T(1,128)} %rows_hbm.1, s32[1,32]{1,0:T(1,128)} %cols_hbm.1, s32[2,128]{1,0:T(2,128)} %bitcast.3), custom_call_target="tpu_custom_call" | custom-call | tf_op jit(solution)/shard_map/pallas_call | solution.py:291
  47.0 0.6 %copy.9 = f32[4,1,8,256]{3,2,1,0:T(8,128)} copy(f32[4,1,8,256]{3,2,1,0:T(8,128)S(1)} %get-tuple-element.8) | data formatting | bytes 65536
  47.6 0.6 %copy.10 = f32[8,4,3]{0,1,2:T(4,128)} copy(f32[8,4,3]{0,1,2:T(4,128)S(1)} %bitcast.2) | data formatting | bytes 768

commit v3 on v2

--- a/solution.py
+++ b/solution.py
@@ -19,7 +19,12 @@
 OWN = WIN * BLK_DEV
 MESH = pl.DeviceIdType.MESH
 PAIRS = [(i, j) for j in range(ITERS + 1) for i in range(j + 1)]
+N_OWNERS = N_GRP * N_DEV
 STAGE_SIZES = (16, 32)
+EARLY = N_GRP // 2
+X_HOPS = (0, 1, 2, 1)
+Y_HOPS = (0, 1, 2, 3, 4, 3, 2, 3)
+FLIPS = sorted(range(1, 32), key=lambda f: -X_HOPS[f // 8] - Y_HOPS[f % 8])
 DISTANCES = [4, -4, 3, -3, 2, -2, 1, -1]
 
 
@@ -58,9 +63,9 @@
 def kernel(
     x_hbm, nb_hbm, rows_hbm, cols_hbm, mirror_hbm, q_ref, h_ref,
     x_ref, nb, rows_ref, cols_ref, mirror_ref,
-    wina, winb, win1, win2, xs, xr, zs, zr, red0, red1,
-    load_sem, swap_send, swap_recv, cross_send, cross_recv, halo_send, halo_recv,
-    zx_send, zx_recv, red_send, red_recv,
+    wina, winb, win1, win2, xs, xr, zs, zr, red0, red1, total_ref,
+    load_sem, swap_send, swap_recv, middle_send, middle_recv, cross_send, cross_recv, halo_send, halo_recv,
+    zx_send, zx_recv, red_send, red_recv, pass_send, pass_recv,
 ):
     side = lax.axis_index("side")
     grp = lax.axis_index("grp")
@@ -68,23 +73,57 @@
     owner = grp * N_DEV + dev
     is_port = side == 0
     chip_x, y_lo, core = dev // 8, (dev // 2) % 4, dev % 2
-    place = (grp * 2 + core, chip_x * 8 + side * 4 + y_lo)
+    is_early = grp < EARLY
+    is_edge = (owner < WIN) | (owner >= N_OWNERS - WIN)
+    column = grp * 2 + core
+    spot = chip_x * 8 + side * 4 + y_lo
+
+    def exists(distance):
+        return (owner + distance >= 0) & (owner + distance < N_OWNERS)
 
     def near(distance, across):
-        other = (owner + distance + N_GRP * N_DEV) % (N_GRP * N_DEV)
+        other = owner + distance
         return (1 - side if across else side, other // N_DEV, other % N_DEV)
 
-    def member(stage, flip):
-        other = place[stage] ^ flip
-        if stage == 0:
-            return (side, other // 2, chip_x * 8 + y_lo * 2 + other % 2)
+    def in_column(flip, half):
+        return (side, half + (grp % EARLY ^ (flip // 2)), chip_x * 8 + y_lo * 2 + (core ^ (flip % 2)))
+
+    def in_plane(flip):
+        other = spot ^ flip
         return ((other // 4) % 2, grp, (other // 8) * 8 + (other % 4) * 2 + core)
 
+    def for_each(items, act, forward=True):
+        @pl.when(jnp.logical_not(is_edge))
+        def _():
+            for _, item in items:
+                act(item)
+
+        @pl.when(is_edge)
+        def _():
+            for d, item in items:
+
+                @pl.when(exists(d if forward else -d))
+                def _(item=item):
+                    act(item)
+
     barrier = pltpu.get_barrier_semaphore()
-    met = [near(d, across) for d in DISTANCES for across in (False, True)]
-    met += [member(s, f) for s in (1, 0) for f in range(1, STAGE_SIZES[s])]
-    for device in met:
+
+    def greet(device):
         pl.semaphore_signal(barrier, inc=1, device_id=device, device_id_type=MESH)
+
+    neighbours = [(d, near(d, across)) for d in DISTANCES for across in (False, True)]
+    partner = (1 - side, grp, dev)
+    greet(partner)
+    for_each(neighbours, greet)
+
+    @pl.when(is_early)
+    def _():
+        for flip in FLIPS:
+            greet(in_plane(flip))
+        for flip in range(1, 8):
+            greet(in_column(flip, 0))
+        for flip in range(8):
+            greet(in_column(flip, EARLY))
 
     loads = [
         pltpu.make_async_copy(source, target, load_sem.at[n])
@@ -113,33 +152,52 @@
         xs[b] = sent
         wina[OWN + b] = sent.astype(jnp.bfloat16)
 
-    pl.semaphore_wait(barrier, len(met))
-
-    copies = []
-
-    def send(source, target, send_sem, recv_sem, device):
-        copy = pltpu.make_async_remote_copy(
+    present = 1
+    for d in DISTANCES:
+        present = present + 2 * exists(d).astype(jnp.int32)
+    pl.semaphore_wait(barrier, present + jnp.where(is_early, len(FLIPS) + 7, 8))
+
+    def remote(source, target, send_sem, recv_sem, device):
+        return pltpu.make_async_remote_copy(
             src_ref=source, dst_ref=target, send_sem=send_sem, recv_sem=recv_sem,
             device_id=device, device_id_type=MESH,
         )
+
+    def start(copy):
         copy.start()
-        copies.append(copy)
-        return copy
-
-    partner = (1 - side, grp, dev)
-    swap = send(xs, xr, swap_send, swap_recv, partner)
-
-    def halo(k, window, target, across, send_sem, recv_sem, n, d):
-        return send(
-            window.at[pl.ds(OWN, BLK_DEV)],
-            target.at[pl.ds((WIN - d) * BLK_DEV, BLK_DEV)],
-            send_sem, recv_sem, near(d, across),
-        )
-
-    hops = []
-    for n, d in enumerate(DISTANCES):
-        hops.append(halo(0, wina, wina, False, halo_send.at[0, n], halo_recv.at[0, n], n, d))
-        hops.append(halo(0, wina, winb, True, cross_send.at[n], cross_recv.at[n], n, d))
+
+    def received(copy):
+        copy.wait_recv()
+
+    def sent_off(copy):
+        copy.wait_send()
+
+    swap = remote(xs, xr, swap_send, swap_recv, partner)
+    copies, hop_copies = [swap], []
+
+    def halo(window, target, across, send_sem, recv_sem):
+        return [
+            (
+                d,
+                remote(
+                    window.at[pl.ds(OWN, BLK_DEV)],
+                    target.at[pl.ds((WIN - d) * BLK_DEV, BLK_DEV)],
+                    send_sem.at[n], recv_sem.at[n], near(d, across),
+                ),
+            )
+            for n, d in enumerate(DISTANCES)
+        ]
+
+    middle = remote(
+        wina.at[pl.ds(OWN, BLK_DEV)], winb.at[pl.ds(OWN, BLK_DEV)], middle_send, middle_recv, partner
+    )
+    start(middle)
+    copies.append(middle)
+    hops = halo(wina, winb, True, cross_send, cross_recv)
+    hops += halo(wina, wina, False, halo_send.at[0], halo_recv.at[0])
+    for_each(hops, start)
+    start(swap)
+    hop_copies += hops
 
     inverse = []
     for b in range(BLK_DEV):
@@ -157,12 +215,7 @@
     sublane = lax.broadcasted_iota(jnp.int32, (NRHS, BLOCK), 0)
     sign = jnp.where(is_port, 1.0, -1.0)
 
-    swap.wait_recv()
     z = [[None] * BLK_DEV for _ in range(ITERS + 1)]
-    for b in range(BLK_DEV):
-        z[0][b] = xr[b] + sign * xs[b]
-        winb[OWN + b] = xr[b].astype(jnp.bfloat16)
-
     for load in loads[2:]:
         load.wait()
     where_from = [
@@ -195,24 +248,27 @@
             window = (None, win1, win2)[k]
             for b in range(BLK_DEV):
                 window[OWN + b] = z[k][b].astype(jnp.bfloat16)
-            hops = [
-                halo(k, window, window, False, halo_send.at[k, n], halo_recv.at[k, n], n, d)
-                for n, d in enumerate(DISTANCES)
-            ]
+            hops = halo(window, window, False, halo_send.at[k], halo_recv.at[k])
+            for_each(hops, start)
+            hop_copies += hops
             for b in range(BLK_DEV):
                 zs[k - 1, b] = z[k][b]
             exchanged.append(
-                send(zs.at[k - 1], zr.at[k - 1], zx_send.at[k - 1], zx_recv.at[k - 1], partner)
+                remote(zs.at[k - 1], zr.at[k - 1], zx_send.at[k - 1], zx_recv.at[k - 1], partner)
             )
-        for copy in hops:
-            copy.wait_recv()
+            start(exchanged[-1])
+        for_each(hops, received, forward=False)
         if k == 0:
+            received(middle)
             total = products([wina, winb])
             total = sign * total[:16] + total[16:]
         else:
             total = products([window])
         z[k + 1] = [total[:NRHS], total[NRHS:]]
 
+    received(swap)
+    for b in range(BLK_DEV):
+        z[0][b] = xr[b] + sign * xs[b]
     partial = jnp.zeros((NRHS, BLOCK), jnp.float32)
     for p, (i, j) in enumerate(PAIRS):
         product = z[i][0] * z[j][0] + z[i][1] * z[j][1]
@@ -221,43 +277,84 @@
         )
     row = jnp.sum(partial, axis=0, keepdims=True)
 
-    for stage, red in enumerate((red0, red1)):
-        size = STAGE_SIZES[stage]
-        red[place[stage]] = row
-        hops = [
-            send(
-                red.at[place[stage]], red.at[place[stage]],
-                red_send.at[stage, flip], red_recv.at[stage, flip], member(stage, flip),
-            )
-            for flip in range(size - 1, 0, -1)
-        ]
-        if stage == 0:
-            for b in range(BLK_DEV):
-                zs[ITERS - 1, b] = z[ITERS][b]
-            exchanged.append(
-                send(
-                    zs.at[ITERS - 1], zr.at[ITERS - 1],
-                    zx_send.at[ITERS - 1], zx_recv.at[ITERS - 1], partner,
-                )
-            )
-        if stage == 1:
-            images = [own]
-            for k in range(ITERS):
-                exchanged[k].wait_recv()
-                image = []
-                for b in range(BLK_DEV):
-                    mine, other = z[k + 1][b], zr[k, b]
-                    port = 0.5 * (mine + other)
-                    starboard = lane_gather(0.5 * (other - mine), inverse[b])
-                    image.append(jnp.where(is_port, port, starboard))
-                images.append(image)
-        for copy in hops:
-            copy.wait_recv()
+    def total_of(red, size):
         parts = [red[n] for n in range(size)]
         while len(parts) > 1:
             parts = [a + b for a, b in zip(parts[::2], parts[1::2], strict=True)]
-        row = parts[0]
-
+        return parts[0]
+
+    red0[column] = row
+
+    def to_column(flip, is_late):
+        kind = 8 * is_late + flip
+        return remote(
+            red0.at[column], red0.at[column], red_send.at[flip], red_recv.at[0, kind], in_column(flip, 0)
+        )
+
+    early_copies = [to_column(flip, 0) for flip in range(8)]
+    late_copies = [to_column(flip, 1) for flip in range(8)]
+
+    @pl.when(is_early)
+    def _():
+        for copy in early_copies[1:]:
+            start(copy)
+
+    @pl.when(jnp.logical_not(is_early))
+    def _():
+        for copy in late_copies:
+            start(copy)
+
+    for b in range(BLK_DEV):
+        zs[ITERS - 1, b] = z[ITERS][b]
+    exchanged.append(
+        remote(
+            zs.at[ITERS - 1], zr.at[ITERS - 1], zx_send.at[ITERS - 1], zx_recv.at[ITERS - 1], partner
+        )
+    )
+    start(exchanged[-1])
+    copies += exchanged
+
+    plane_copies = [
+        remote(red1.at[spot], red1.at[spot], red_send.at[flip], red_recv.at[1, flip], in_plane(flip))
+        for flip in FLIPS
+    ]
+    pass_on = remote(
+        total_ref, total_ref, pass_send, pass_recv, (side, grp % EARLY + EARLY, dev)
+    )
+
+    @pl.when(is_early)
+    def _():
+        for copy in early_copies[1:] + late_copies:
+            received(copy)
+        for copy in early_copies[1:]:
+            sent_off(copy)
+        red1[spot] = total_of(red0, STAGE_SIZES[0])
+        for copy in plane_copies:
+            start(copy)
+
+    images = [own]
+    for k in range(ITERS):
+        received(exchanged[k])
+        image = []
+        for b in range(BLK_DEV):
+            mine, other = z[k + 1][b], zr[k, b]
+            port = 0.5 * (mine + other)
+            starboard = lane_gather(0.5 * (other - mine), inverse[b])
+            image.append(jnp.where(is_port, port, starboard))
+        images.append(image)
+
+    @pl.when(is_early)
+    def _():
+        for copy in plane_copies:
+            received(copy)
+        total_ref[...] = total_of(red1, STAGE_SIZES[1])
+        start(pass_on)
+
+    @pl.when(jnp.logical_not(is_early))
+    def _():
+        received(pass_on)
+
+    row = total_ref[...]
     spread = jnp.broadcast_to(row * (0.5 / TOTAL_PANELS), (NRHS, BLOCK))
     gram = {}
     for p, pair in enumerate(PAIRS):
@@ -277,7 +374,30 @@
     for k in range(ITERS):
         h_ref[k] = turned[k * (ITERS + 1) : (k + 1) * (ITERS + 1), :]
     for copy in copies:
-        copy.wait_send()
+        sent_off(copy)
+    for_each(hop_copies, sent_off)
+
+    @pl.when(is_early)
+    def _():
+        for copy in plane_copies:
+            sent_off(copy)
+        sent_off(pass_on)
+
+    @pl.when(jnp.logical_not(is_early))
+    def _():
+        for copy in late_copies:
+            sent_off(copy)
+
+
+def settle(q_ref, h_ref, q_out, h_out, sem):
+    moves = [
+        pltpu.make_async_copy(q_ref, q_out, sem.at[0]),
+        pltpu.make_async_copy(h_ref, h_out, sem.at[1]),
+    ]
+    for move in moves:
+        move.start()
+    for move in moves:
+        move.wait()
 
 
 def on_device(sources, near_blocks, block_rows, block_cols, mirror):
@@ -306,12 +426,15 @@
             blocks, blocks,
             steps, steps,
             *[pltpu.VMEM((size, 1, BLOCK), f32) for size in STAGE_SIZES],
+            pltpu.VMEM((1, BLOCK), f32),
             dma((5,)),
+            dma, dma,
             dma, dma,
             dma((2 * WIN,)), dma((2 * WIN,)),
             dma((ITERS, 2 * WIN)), dma((ITERS, 2 * WIN)),
             dma((ITERS,)), dma((ITERS,)),
-            dma((2, 32)), dma((2, 32)),
+            dma((32,)), dma((2, 32)),
+            dma, dma,
         ],
         compiler_params=pltpu.CompilerParams(
             collective_id=0, has_side_effects=True, vmem_limit_bytes=8 * 1024 * 1024
@@ -324,6 +447,17 @@
             )
         ]
     )
+    q, h = pl.pallas_call(
+        settle,
+        out_shape=(
+            jax.ShapeDtypeStruct(q.shape, f32),
+            jax.ShapeDtypeStruct(h.shape, f32),
+        ),
+        in_specs=[vmem, vmem],
+        out_specs=(hbm, hbm),
+        scratch_shapes=[dma((2,))],
+        compiler_params=pltpu.CompilerParams(vmem_limit_bytes=8 * 1024 * 1024),
+    )(q, h)
     return q, jnp.transpose(h)
 
 

time: 48.4 us -> 47.1 us (0.973); the launches traced: 48.2 us -> 46.4 us
  local copies, waits for them, and re-layouts: 1.21 us -> 0 us
  Pallas kernels: 46.4 us -> 45.8 us
    pallas_call x1, Pallas kernels: 46.4 us -> 45.1 us  [on_device(): pl.pallas_call(kernel, out_shape=(jax.ShapeDtypeStruct((ITERS + 1, 1, NRH...]
    unnamed x2 -> x0, local copies, waits for them, and re-layouts: 1.21 us -> none
    pallas_call x0 -> x1, Pallas kernels: none -> 0.64 us  [on_device(): pl.pallas_call(settle, out_shape=(jax.ShapeDtypeStruct(q.shape, f32), jax...]
where the time goes in v3:
time: 47.1 us; the launch traced here: 46.4 us
  Pallas kernels  45.8 us (97%)
  between operations  0.64 us (1%)
    pallas_call x1, Pallas kernels, on_device(): pl.pallas_call(kernel, out_shape=(jax.ShapeDtypeStruct((ITERS + 1, 1, NRH...  45.1 us

profile of v3, /device:TPU:1, one launch (start us, length us, event | category | flops | bytes accessed | tf_op | source)
XLA Modules:
  0.0 46.4 jit_solution(17005753016758956295)
XLA Ops:
  0.6 45.1 %shard_map.68 = (f32[4,1,8,256]{3,2,1,0:T(8,128)S(1)}, f32[3,4,8]{2,1,0:T(4,128)S(1)}) custom-call(f32[1,8,256]{2,1,0:T(8,128)} %x_hbm.1, bf16[1,32,128,128]{3,2,1,0:T(8,128)(2,1)} %nb_hbm.1, s32[1,32]{1,0:T(1,128)} %rows_hbm.1, s32[1,32]{1,0:T(1,128)} %cols_hbm.1, s32[2,128]{1,0:T(2,128)} %bitcast.2), custom_call_target="tpu_custom_call" | custom-call | tf_op jit(solution)/shard_map/pallas_call | solution.py:411
  45.8 0.6 %shard_map.69 = (f32[4,1,8,256]{3,2,1,0:T(8,128)}, f32[3,4,8]{2,1,0:T(4,128)}) custom-call(f32[4,1,8,256]{3,2,1,0:T(8,128)S(1)} %get-tuple-element.6.q_ref, f32[3,4,8]{2,1,0:T(4,128)S(1)} %get-tuple-element.7.h_ref), custom_call_target="tpu_custom_call" | custom-call | tf_op jit(solution)/shard_map/pallas_call | solution.py:450

commit v4 on v3

--- a/solution.py
+++ b/solution.py
@@ -81,6 +81,8 @@
     def exists(distance):
         return (owner + distance >= 0) & (owner + distance < N_OWNERS)
 
+    partner = (1 - side, grp, dev)
+
     def near(distance, across):
         other = owner + distance
         return (1 - side if across else side, other // N_DEV, other % N_DEV)
@@ -112,7 +114,6 @@
         pl.semaphore_signal(barrier, inc=1, device_id=device, device_id_type=MESH)
 
     neighbours = [(d, near(d, across)) for d in DISTANCES for across in (False, True)]
-    partner = (1 - side, grp, dev)
     greet(partner)
     for_each(neighbours, greet)
 
@@ -175,27 +176,41 @@
     swap = remote(xs, xr, swap_send, swap_recv, partner)
     copies, hop_copies = [swap], []
 
-    def halo(window, target, across, send_sem, recv_sem):
+    def halo(window, target, across, send_sem, recv_sem, distances):
         return [
             (
                 d,
                 remote(
                     window.at[pl.ds(OWN, BLK_DEV)],
                     target.at[pl.ds((WIN - d) * BLK_DEV, BLK_DEV)],
-                    send_sem.at[n], recv_sem.at[n], near(d, across),
+                    send_sem.at[WIN + d], recv_sem.at[WIN + d], near(d, across),
                 ),
             )
-            for n, d in enumerate(DISTANCES)
+            for d in distances
         ]
+
+    outward = jnp.where(y_lo >= 2, 1, -1)
+    far_first = [outward * d for d in range(WIN, 0, -1)]
+    near_last = [outward * -d for d in range(WIN, 0, -1)]
 
     middle = remote(
         wina.at[pl.ds(OWN, BLK_DEV)], winb.at[pl.ds(OWN, BLK_DEV)], middle_send, middle_recv, partner
     )
     start(middle)
     copies.append(middle)
-    hops = halo(wina, winb, True, cross_send, cross_recv)
-    hops += halo(wina, wina, False, halo_send.at[0], halo_recv.at[0])
-    for_each(hops, start)
+
+    def over_there(distances):
+        return halo(wina, winb, True, cross_send, cross_recv, distances)
+
+    def over_here(distances):
+        return halo(wina, wina, False, halo_send.at[0], halo_recv.at[0], distances)
+
+    for_each(
+        over_there([1, -1]) + over_here(far_first) + over_there([2, -2, 3, -3, 4, -4])
+        + over_here(near_last),
+        start,
+    )
+    hops = over_there(DISTANCES) + over_here(DISTANCES)
     start(swap)
     hop_copies += hops
 
@@ -222,6 +237,9 @@
         jnp.clip(cols_ref[0, e] - (owner - WIN) * BLK_DEV, 0, SLOTS - 1) for e in range(NB_DEV)
     ]
     upper = [(rows_ref[0, e] == 0).astype(jnp.float32) for e in range(NB_DEV)]
+
+    for e in range(NB_DEV):
+        nb[e] = jnp.transpose(nb[e])
 
     def products(windows):
         total = jnp.zeros((16 * len(windows), BLOCK), jnp.float32)
@@ -236,8 +254,8 @@
                 rights.append(nb[f])
             total = total + lax.dot_general(
                 jnp.concatenate(lefts, axis=1),
-                jnp.concatenate(rights, axis=1),
-                (((1,), (1,)), ((), ())),
+                jnp.concatenate(rights, axis=0),
+                (((1,), (0,)), ((), ())),
                 preferred_element_type=jnp.float32,
             )
         return total
@@ -248,8 +266,11 @@
             window = (None, win1, win2)[k]
             for b in range(BLK_DEV):
                 window[OWN + b] = z[k][b].astype(jnp.bfloat16)
-            hops = halo(window, window, False, halo_send.at[k], halo_recv.at[k])
-            for_each(hops, start)
+            for_each(
+                halo(window, window, False, halo_send.at[k], halo_recv.at[k], far_first + near_last),
+                start,
+            )
+            hops = halo(window, window, False, halo_send.at[k], halo_recv.at[k], DISTANCES)
             hop_copies += hops
             for b in range(BLK_DEV):
                 zs[k - 1, b] = z[k][b]
@@ -430,8 +451,8 @@
             dma((5,)),
             dma, dma,
             dma, dma,
-            dma((2 * WIN,)), dma((2 * WIN,)),
-            dma((ITERS, 2 * WIN)), dma((ITERS, 2 * WIN)),
+            dma((2 * WIN + 1,)), dma((2 * WIN + 1,)),
+            dma((ITERS, 2 * WIN + 1)), dma((ITERS, 2 * WIN + 1)),
             dma((ITERS,)), dma((ITERS,)),
             dma((32,)), dma((2, 32)),
             dma, dma,

time: 47.1 us -> 46 us (0.977)
  Pallas kernels: 45.8 us -> 44.6 us
    pallas_call x1, Pallas kernels: 45.1 us -> 43.9 us  [on_device(): pl.pallas_call(kernel, out_shape=(jax.ShapeDtypeStruct((ITERS + 1, 1, NRH...]
where the time goes in v4:
time: 46 us; the launch traced here: 45.2 us
  Pallas kernels  44.6 us (97%)
  between operations  0.64 us (1%)
    pallas_call x1, Pallas kernels, on_device(): pl.pallas_call(kernel, out_shape=(jax.ShapeDtypeStruct((ITERS + 1, 1, NRH...  43.9 us

profile of v4, /device:TPU:1, one launch (start us, length us, event | category | flops | bytes accessed | tf_op | source)
XLA Modules:
  0.0 45.2 jit_solution(4213408291792668083)
XLA Ops:
  0.6 43.9 %shard_map.68 = (f32[4,1,8,256]{3,2,1,0:T(8,128)S(1)}, f32[3,4,8]{2,1,0:T(4,128)S(1)}) custom-call(f32[1,8,256]{2,1,0:T(8,128)} %x_hbm.1, bf16[1,32,128,128]{3,2,1,0:T(8,128)(2,1)} %nb_hbm.1, s32[1,32]{1,0:T(1,128)} %rows_hbm.1, s32[1,32]{1,0:T(1,128)} %cols_hbm.1, s32[2,128]{1,0:T(2,128)} %bitcast.2), custom_call_target="tpu_custom_call" | custom-call | tf_op jit(solution)/shard_map/pallas_call | solution.py:432
  44.6 0.6 %shard_map.69 = (f32[4,1,8,256]{3,2,1,0:T(8,128)}, f32[3,4,8]{2,1,0:T(4,128)}) custom-call(f32[4,1,8,256]{3,2,1,0:T(8,128)S(1)} %get-tuple-element.6.q_ref, f32[3,4,8]{2,1,0:T(4,128)S(1)} %get-tuple-element.7.h_ref), custom_call_target="tpu_custom_call" | custom-call | tf_op jit(solution)/shard_map/pallas_call | solution.py:471

commit v5 on v4

--- a/solution.py
+++ b/solution.py
@@ -260,6 +260,16 @@
             )
         return total
 
+    def with_pairs(partial, pairs):
+        for i, j in pairs:
+            product = z[i][0] * z[j][0] + z[i][1] * z[j][1]
+            partial = jnp.where(
+                lane == PAIRS.index((i, j)) * NRHS + sublane,
+                jnp.sum(product, axis=1, keepdims=True),
+                partial,
+            )
+        return partial
+
     exchanged = []
     for k in range(ITERS):
         if k > 0:
@@ -278,6 +288,13 @@
                 remote(zs.at[k - 1], zr.at[k - 1], zx_send.at[k - 1], zx_recv.at[k - 1], partner)
             )
             start(exchanged[-1])
+        if k == ITERS - 1:
+            received(swap)
+            for b in range(BLK_DEV):
+                z[0][b] = xr[b] + sign * xs[b]
+            partial = with_pairs(
+                jnp.zeros((NRHS, BLOCK), jnp.float32), [p for p in PAIRS if p[1] < ITERS]
+            )
         for_each(hops, received, forward=False)
         if k == 0:
             received(middle)
@@ -287,15 +304,7 @@
             total = products([window])
         z[k + 1] = [total[:NRHS], total[NRHS:]]
 
-    received(swap)
-    for b in range(BLK_DEV):
-        z[0][b] = xr[b] + sign * xs[b]
-    partial = jnp.zeros((NRHS, BLOCK), jnp.float32)
-    for p, (i, j) in enumerate(PAIRS):
-        product = z[i][0] * z[j][0] + z[i][1] * z[j][1]
-        partial = jnp.where(
-            lane == p * NRHS + sublane, jnp.sum(product, axis=1, keepdims=True), partial
-        )
+    partial = with_pairs(partial, [p for p in PAIRS if p[1] == ITERS])
     row = jnp.sum(partial, axis=0, keepdims=True)
 
     def total_of(red, size):
@@ -322,8 +331,9 @@
 
     @pl.when(jnp.logical_not(is_early))
     def _():
-        for copy in late_copies:
-            start(copy)
+        for z_to in range(EARLY):
+            for core_flip in range(2):
+                start(to_column((grp % EARLY ^ z_to) * 2 + core_flip, 1))
 
     for b in range(BLK_DEV):
         zs[ITERS - 1, b] = z[ITERS][b]
@@ -335,13 +345,18 @@
     start(exchanged[-1])
     copies += exchanged
 
-    plane_copies = [
-        remote(red1.at[spot], red1.at[spot], red_send.at[flip], red_recv.at[1, flip], in_plane(flip))
-        for flip in FLIPS
+    def to_plane(flip):
+        return remote(
+            red1.at[spot], red1.at[spot], red_send.at[flip], red_recv.at[1, flip], in_plane(flip)
+        )
+
+    plane_copies = [to_plane(flip) for flip in range(1, 32)]
+
+    passes = grp == EARLY - 1
+    pass_on = [
+        remote(total_ref, total_ref, pass_send.at[n], pass_recv, (side, EARLY + n, dev))
+        for n in range(N_GRP - EARLY)
     ]
-    pass_on = remote(
-        total_ref, total_ref, pass_send, pass_recv, (side, grp % EARLY + EARLY, dev)
-    )
 
     @pl.when(is_early)
     def _():
@@ -350,8 +365,15 @@
         for copy in early_copies[1:]:
             sent_off(copy)
         red1[spot] = total_of(red0, STAGE_SIZES[0])
-        for copy in plane_copies:
-            start(copy)
+        for y_to in (0, 1, 2, 3, 7, 4, 5, 6):
+            y_flip = spot % 8 ^ y_to
+            for x_flip in (2, 1, 3):
+                start(to_plane(x_flip * 8 + y_flip))
+
+            @pl.when(y_flip > 0)
+            def _(y_flip=y_flip):
+                start(to_plane(y_flip))
+
 
     images = [own]
     for k in range(ITERS):
@@ -369,11 +391,15 @@
         for copy in plane_copies:
             received(copy)
         total_ref[...] = total_of(red1, STAGE_SIZES[1])
-        start(pass_on)
+
+    @pl.when(passes)
+    def _():
+        for copy in pass_on:
+            start(copy)
 
     @pl.when(jnp.logical_not(is_early))
     def _():
-        received(pass_on)
+        received(pass_on[0])
 
     row = total_ref[...]
     spread = jnp.broadcast_to(row * (0.5 / TOTAL_PANELS), (NRHS, BLOCK))
@@ -402,7 +428,11 @@
     def _():
         for copy in plane_copies:
             sent_off(copy)
-        sent_off(pass_on)
+
+    @pl.when(passes)
+    def _():
+        for copy in pass_on:
+            sent_off(copy)
 
     @pl.when(jnp.logical_not(is_early))
     def _():
@@ -455,7 +485,7 @@
             dma((ITERS, 2 * WIN + 1)), dma((ITERS, 2 * WIN + 1)),
             dma((ITERS,)), dma((ITERS,)),
             dma((32,)), dma((2, 32)),
-            dma, dma,
+            dma((N_GRP - EARLY,)), dma,
         ],
         compiler_params=pltpu.CompilerParams(
             collective_id=0, has_side_effects=True, vmem_limit_bytes=8 * 1024 * 1024

time: 46 us -> 45.1 us (0.980); the launches traced: 45.2 us -> 44.9 us
  no operation moved by 1% of the time
where the time goes in v5:
time: 45.1 us; the launch traced here: 44.9 us
  Pallas kernels  44.3 us (98%)
  between operations  0.64 us (1%)
    pallas_call x1, Pallas kernels, on_device(): pl.pallas_call(kernel, out_shape=(jax.ShapeDtypeStruct((ITERS + 1, 1, NRH...  43.6 us

profile of v5, /device:TPU:1, one launch (start us, length us, event | category | flops | bytes accessed | tf_op | source)
XLA Modules:
  0.0 44.9 jit_solution(9359041311531931017)
XLA Ops:
  0.6 43.6 %shard_map.68 = (f32[4,1,8,256]{3,2,1,0:T(8,128)S(1)}, f32[3,4,8]{2,1,0:T(4,128)S(1)}) custom-call(f32[1,8,256]{2,1,0:T(8,128)} %x_hbm.1, bf16[1,32,128,128]{3,2,1,0:T(8,128)(2,1)} %nb_hbm.1, s32[1,32]{1,0:T(1,128)} %rows_hbm.1, s32[1,32]{1,0:T(1,128)} %cols_hbm.1, s32[2,128]{1,0:T(2,128)} %bitcast.2), custom_call_target="tpu_custom_call" | custom-call | tf_op jit(solution)/shard_map/pallas_call | solution.py:462
  44.3 0.6 %shard_map.69 = (f32[4,1,8,256]{3,2,1,0:T(8,128)}, f32[3,4,8]{2,1,0:T(4,128)}) custom-call(f32[4,1,8,256]{3,2,1,0:T(8,128)S(1)} %get-tuple-element.6.q_ref, f32[3,4,8]{2,1,0:T(4,128)S(1)} %get-tuple-element.7.h_ref), custom_call_target="tpu_custom_call" | custom-call | tf_op jit(solution)/shard_map/pallas_call | solution.py:501

commit v6 on v5

--- a/solution.py
+++ b/solution.py
@@ -64,7 +64,7 @@
     x_hbm, nb_hbm, rows_hbm, cols_hbm, mirror_hbm, q_ref, h_ref,
     x_ref, nb, rows_ref, cols_ref, mirror_ref,
     wina, winb, win1, win2, xs, xr, zs, zr, red0, red1, total_ref,
-    load_sem, swap_send, swap_recv, middle_send, middle_recv, cross_send, cross_recv, halo_send, halo_recv,
+    load_sem, swap_send, swap_recv, cross_send, cross_recv, halo_send, halo_recv,
     zx_send, zx_recv, red_send, red_recv, pass_send, pass_recv,
 ):
     side = lax.axis_index("side")
@@ -94,7 +94,7 @@
         other = spot ^ flip
         return ((other // 4) % 2, grp, (other // 8) * 8 + (other % 4) * 2 + core)
 
-    def for_each(items, act, forward=True):
+    def for_each(items, act):
         @pl.when(jnp.logical_not(is_edge))
         def _():
             for _, item in items:
@@ -104,9 +104,30 @@
         def _():
             for d, item in items:
 
-                @pl.when(exists(d if forward else -d))
+                @pl.when(exists(d))
                 def _(item=item):
                     act(item)
+
+    n_near = 0
+    for d in DISTANCES:
+        n_near = n_near + exists(d).astype(jnp.int32)
+
+    def wait_bytes(ref, count, sem):
+        part = ref.at[pl.ds(0, count)]
+        pltpu.make_async_copy(part, part, sem).wait()
+
+    def wait_near(ref, sem, extra=0):
+        @pl.when(jnp.logical_not(is_edge))
+        def _():
+            wait_bytes(ref, (2 * WIN + extra) * BLK_DEV, sem)
+
+        @pl.when(is_edge)
+        def _():
+            for m in range(WIN, 2 * WIN):
+
+                @pl.when(n_near == m)
+                def _(m=m):
+                    wait_bytes(ref, (m + extra) * BLK_DEV, sem)
 
     barrier = pltpu.get_barrier_semaphore()
 
@@ -153,10 +174,7 @@
         xs[b] = sent
         wina[OWN + b] = sent.astype(jnp.bfloat16)
 
-    present = 1
-    for d in DISTANCES:
-        present = present + 2 * exists(d).astype(jnp.int32)
-    pl.semaphore_wait(barrier, present + jnp.where(is_early, len(FLIPS) + 7, 8))
+    pl.semaphore_wait(barrier, 1 + 2 * n_near + jnp.where(is_early, len(FLIPS) + 7, 8))
 
     def remote(source, target, send_sem, recv_sem, device):
         return pltpu.make_async_remote_copy(
@@ -174,7 +192,7 @@
         copy.wait_send()
 
     swap = remote(xs, xr, swap_send, swap_recv, partner)
-    copies, hop_copies = [swap], []
+    copies = [swap]
 
     def halo(window, target, across, send_sem, recv_sem, distances):
         return [
@@ -183,7 +201,7 @@
                 remote(
                     window.at[pl.ds(OWN, BLK_DEV)],
                     target.at[pl.ds((WIN - d) * BLK_DEV, BLK_DEV)],
-                    send_sem.at[WIN + d], recv_sem.at[WIN + d], near(d, across),
+                    send_sem, recv_sem, near(d, across),
                 ),
             )
             for d in distances
@@ -194,10 +212,9 @@
     near_last = [outward * -d for d in range(WIN, 0, -1)]
 
     middle = remote(
-        wina.at[pl.ds(OWN, BLK_DEV)], winb.at[pl.ds(OWN, BLK_DEV)], middle_send, middle_recv, partner
+        wina.at[pl.ds(OWN, BLK_DEV)], winb.at[pl.ds(OWN, BLK_DEV)], cross_send, cross_recv, partner
     )
     start(middle)
-    copies.append(middle)
 
     def over_there(distances):
         return halo(wina, winb, True, cross_send, cross_recv, distances)
@@ -210,9 +227,7 @@
         + over_here(near_last),
         start,
     )
-    hops = over_there(DISTANCES) + over_here(DISTANCES)
     start(swap)
-    hop_copies += hops
 
     inverse = []
     for b in range(BLK_DEV):
@@ -280,8 +295,6 @@
                 halo(window, window, False, halo_send.at[k], halo_recv.at[k], far_first + near_last),
                 start,
             )
-            hops = halo(window, window, False, halo_send.at[k], halo_recv.at[k], DISTANCES)
-            hop_copies += hops
             for b in range(BLK_DEV):
                 zs[k - 1, b] = z[k][b]
             exchanged.append(
@@ -295,9 +308,9 @@
             partial = with_pairs(
                 jnp.zeros((NRHS, BLOCK), jnp.float32), [p for p in PAIRS if p[1] < ITERS]
             )
-        for_each(hops, received, forward=False)
+        wait_near(wina if k == 0 else window, halo_recv.at[k])
         if k == 0:
-            received(middle)
+            wait_near(winb, cross_recv, 1)
             total = products([wina, winb])
             total = sign * total[:16] + total[16:]
         else:
@@ -315,14 +328,12 @@
 
     red0[column] = row
 
-    def to_column(flip, is_late):
-        kind = 8 * is_late + flip
+    def to_column(flip):
         return remote(
-            red0.at[column], red0.at[column], red_send.at[flip], red_recv.at[0, kind], in_column(flip, 0)
+            red0.at[column], red0.at[column], red_send.at[0], red_recv.at[0], in_column(flip, 0)
         )
 
-    early_copies = [to_column(flip, 0) for flip in range(8)]
-    late_copies = [to_column(flip, 1) for flip in range(8)]
+    early_copies = [to_column(flip) for flip in range(8)]
 
     @pl.when(is_early)
     def _():
@@ -333,7 +344,7 @@
     def _():
         for z_to in range(EARLY):
             for core_flip in range(2):
-                start(to_column((grp % EARLY ^ z_to) * 2 + core_flip, 1))
+                start(to_column((grp % EARLY ^ z_to) * 2 + core_flip))
 
     for b in range(BLK_DEV):
         zs[ITERS - 1, b] = z[ITERS][b]
@@ -347,10 +358,8 @@
 
     def to_plane(flip):
         return remote(
-            red1.at[spot], red1.at[spot], red_send.at[flip], red_recv.at[1, flip], in_plane(flip)
+            red1.at[spot], red1.at[spot], red_send.at[1], red_recv.at[1], in_plane(flip)
         )
-
-    plane_copies = [to_plane(flip) for flip in range(1, 32)]
 
     passes = grp == EARLY - 1
     pass_on = [
@@ -360,10 +369,7 @@
 
     @pl.when(is_early)
     def _():
-        for copy in early_copies[1:] + late_copies:
-            received(copy)
-        for copy in early_copies[1:]:
-            sent_off(copy)
+        wait_bytes(red0, STAGE_SIZES[0] - 1, red_recv.at[0])
         red1[spot] = total_of(red0, STAGE_SIZES[0])
         for y_to in (0, 1, 2, 3, 7, 4, 5, 6):
             y_flip = spot % 8 ^ y_to
@@ -386,10 +392,23 @@
             image.append(jnp.where(is_port, port, starboard))
         images.append(image)
 
+    for copy in copies:
+        sent_off(copy)
+    wait_near(winb, cross_send, 1)
+    for k, window in enumerate((wina, win1, win2)):
+        wait_near(window, halo_send.at[k])
+
     @pl.when(is_early)
     def _():
-        for copy in plane_copies:
-            received(copy)
+        wait_bytes(red0, 7, red_send.at[0])
+
+    @pl.when(jnp.logical_not(is_early))
+    def _():
+        wait_bytes(red0, 8, red_send.at[0])
+
+    @pl.when(is_early)
+    def _():
+        wait_bytes(red1, STAGE_SIZES[1] - 1, red_recv.at[1])
         total_ref[...] = total_of(red1, STAGE_SIZES[1])
 
     @pl.when(passes)
@@ -420,23 +439,14 @@
     turned = jnp.transpose(table)
     for k in range(ITERS):
         h_ref[k] = turned[k * (ITERS + 1) : (k + 1) * (ITERS + 1), :]
-    for copy in copies:
-        sent_off(copy)
-    for_each(hop_copies, sent_off)
 
     @pl.when(is_early)
     def _():
-        for copy in plane_copies:
-            sent_off(copy)
+        wait_bytes(red1, STAGE_SIZES[1] - 1, red_send.at[1])
 
     @pl.when(passes)
     def _():
         for copy in pass_on:
-            sent_off(copy)
-
-    @pl.when(jnp.logical_not(is_early))
-    def _():
-        for copy in late_copies:
             sent_off(copy)
 
 
@@ -481,10 +491,9 @@
             dma((5,)),
             dma, dma,
             dma, dma,
-            dma((2 * WIN + 1,)), dma((2 * WIN + 1,)),
-            dma((ITERS, 2 * WIN + 1)), dma((ITERS, 2 * WIN + 1)),
             dma((ITERS,)), dma((ITERS,)),
-            dma((32,)), dma((2, 32)),
+            dma((ITERS,)), dma((ITERS,)),
+            dma((2,)), dma((2,)),
             dma((N_GRP - EARLY,)), dma,
         ],
         compiler_params=pltpu.CompilerParams(

time: 45.1 us -> 43.4 us (0.962)
  Pallas kernels: 44.3 us -> 42.6 us
    pallas_call x1, Pallas kernels: 43.6 us -> 42 us  [on_device(): pl.pallas_call(kernel, out_shape=(jax.ShapeDtypeStruct((ITERS + 1, 1, NRH...]
where the time goes in v6:
time: 43.4 us; the launch traced here: 43.2 us
  Pallas kernels  42.6 us (98%)
  between operations  0.64 us (1%)
    pallas_call x1, Pallas kernels, on_device(): pl.pallas_call(kernel, out_shape=(jax.ShapeDtypeStruct((ITERS + 1, 1, NRH...  42 us

profile of v6, /device:TPU:1, one launch (start us, length us, event | category | flops | bytes accessed | tf_op | source)
XLA Modules:
  0.0 43.2 jit_solution(3287730708992234153)
XLA Ops:
  0.6 42.0 %shard_map.68 = (f32[4,1,8,256]{3,2,1,0:T(8,128)S(1)}, f32[3,4,8]{2,1,0:T(4,128)S(1)}) custom-call(f32[1,8,256]{2,1,0:T(8,128)} %x_hbm.1, bf16[1,32,128,128]{3,2,1,0:T(8,128)(2,1)} %nb_hbm.1, s32[1,32]{1,0:T(1,128)} %rows_hbm.1, s32[1,32]{1,0:T(1,128)} %cols_hbm.1, s32[2,128]{1,0:T(2,128)} %bitcast.2), custom_call_target="tpu_custom_call" | custom-call | tf_op jit(solution)/shard_map/pallas_call | solution.py:472
  42.6 0.6 %shard_map.69 = (f32[4,1,8,256]{3,2,1,0:T(8,128)}, f32[3,4,8]{2,1,0:T(4,128)}) custom-call(f32[4,1,8,256]{3,2,1,0:T(8,128)S(1)} %get-tuple-element.6.q_ref, f32[3,4,8]{2,1,0:T(4,128)S(1)} %get-tuple-element.7.h_ref), custom_call_target="tpu_custom_call" | custom-call | tf_op jit(solution)/shard_map/pallas_call | solution.py:510

commit v7 on v6

--- a/solution.py
+++ b/solution.py
@@ -56,7 +56,8 @@
                 u[i] = u[i] - h[(j, k)] * c[j][i]
         norm = jnp.sqrt(jnp.maximum(dot(u, u), 0.0) + EPSILON)
         h[(k + 1, k)] = norm
-        c.append([v / norm for v in u])
+        inverse = 1.0 / norm
+        c.append([v * inverse for v in u])
     return c, h
 
 
@@ -129,24 +130,6 @@
                 def _(m=m):
                     wait_bytes(ref, (m + extra) * BLK_DEV, sem)
 
-    barrier = pltpu.get_barrier_semaphore()
-
-    def greet(device):
-        pl.semaphore_signal(barrier, inc=1, device_id=device, device_id_type=MESH)
-
-    neighbours = [(d, near(d, across)) for d in DISTANCES for across in (False, True)]
-    greet(partner)
-    for_each(neighbours, greet)
-
-    @pl.when(is_early)
-    def _():
-        for flip in FLIPS:
-            greet(in_plane(flip))
-        for flip in range(1, 8):
-            greet(in_column(flip, 0))
-        for flip in range(8):
-            greet(in_column(flip, EARLY))
-
     loads = [
         pltpu.make_async_copy(source, target, load_sem.at[n])
         for n, (source, target) in enumerate(
@@ -161,6 +144,25 @@
     ]
     for load in loads:
         load.start()
+
+    barrier = pltpu.get_barrier_semaphore()
+
+    def greet(device):
+        pl.semaphore_signal(barrier, inc=1, device_id=device, device_id_type=MESH)
+
+    neighbours = [(d, near(d, across)) for d in DISTANCES for across in (False, True)]
+    greet(partner)
+    for_each(neighbours, greet)
+
+    @pl.when(is_early)
+    def _():
+        for flip in FLIPS:
+            greet(in_plane(flip))
+        for flip in range(1, 8):
+            greet(in_column(flip, 0))
+        for flip in range(8):
+            greet(in_column(flip, EARLY))
+
     loads[0].wait()
     loads[1].wait()
 
@@ -285,7 +287,6 @@
             )
         return partial
 
-    exchanged = []
     for k in range(ITERS):
         if k > 0:
             window = (None, win1, win2)[k]
@@ -297,10 +298,6 @@
             )
             for b in range(BLK_DEV):
                 zs[k - 1, b] = z[k][b]
-            exchanged.append(
-                remote(zs.at[k - 1], zr.at[k - 1], zx_send.at[k - 1], zx_recv.at[k - 1], partner)
-            )
-            start(exchanged[-1])
         if k == ITERS - 1:
             received(swap)
             for b in range(BLK_DEV):
@@ -348,13 +345,9 @@
 
     for b in range(BLK_DEV):
         zs[ITERS - 1, b] = z[ITERS][b]
-    exchanged.append(
-        remote(
-            zs.at[ITERS - 1], zr.at[ITERS - 1], zx_send.at[ITERS - 1], zx_recv.at[ITERS - 1], partner
-        )
-    )
-    start(exchanged[-1])
-    copies += exchanged
+    exchange = remote(zs, zr, zx_send, zx_recv, partner)
+    start(exchange)
+    copies.append(exchange)
 
     def to_plane(flip):
         return remote(
@@ -381,9 +374,9 @@
                 start(to_plane(y_flip))
 
 
+    received(exchange)
     images = [own]
     for k in range(ITERS):
-        received(exchanged[k])
         image = []
         for b in range(BLK_DEV):
             mine, other = z[k + 1][b], zr[k, b]
@@ -409,10 +402,10 @@
     @pl.when(is_early)
     def _():
         wait_bytes(red1, STAGE_SIZES[1] - 1, red_recv.at[1])
+
+    @pl.when(passes)
+    def _():
         total_ref[...] = total_of(red1, STAGE_SIZES[1])
-
-    @pl.when(passes)
-    def _():
         for copy in pass_on:
             start(copy)
 
@@ -420,7 +413,7 @@
     def _():
         received(pass_on[0])
 
-    row = total_ref[...]
+    row = jnp.where(is_early, total_of(red1, STAGE_SIZES[1]), total_ref[...])
     spread = jnp.broadcast_to(row * (0.5 / TOTAL_PANELS), (NRHS, BLOCK))
     gram = {}
     for p, pair in enumerate(PAIRS):
@@ -492,7 +485,7 @@
             dma, dma,
             dma, dma,
             dma((ITERS,)), dma((ITERS,)),
-            dma((ITERS,)), dma((ITERS,)),
+            dma, dma,
             dma((2,)), dma((2,)),
             dma((N_GRP - EARLY,)), dma,
         ],

time: 43.4 us -> 43.3 us (level)
  no operation moved by 1% of the time
where the time goes in v7:
time: 43.3 us; the launch traced here: 43.2 us
  Pallas kernels  42.6 us (98%)
  between operations  0.64 us (1%)
    pallas_call x1, Pallas kernels, on_device(): pl.pallas_call(kernel, out_shape=(jax.ShapeDtypeStruct((ITERS + 1, 1, NRH...  41.9 us

profile of v7, /device:TPU:1, one launch (start us, length us, event | category | flops | bytes accessed | tf_op | source)
XLA Modules:
  0.0 43.2 jit_solution(14354469148487810892)
XLA Ops:
  0.6 41.9 %shard_map.68 = (f32[4,1,8,256]{3,2,1,0:T(8,128)S(1)}, f32[3,4,8]{2,1,0:T(4,128)S(1)}) custom-call(f32[1,8,256]{2,1,0:T(8,128)} %x_hbm.1, bf16[1,32,128,128]{3,2,1,0:T(8,128)(2,1)} %nb_hbm.1, s32[1,32]{1,0:T(1,128)} %rows_hbm.1, s32[1,32]{1,0:T(1,128)} %cols_hbm.1, s32[2,128]{1,0:T(2,128)} %bitcast.2), custom_call_target="tpu_custom_call" | custom-call | tf_op jit(solution)/shard_map/pallas_call | solution.py:465
  42.6 0.6 %shard_map.69 = (f32[4,1,8,256]{3,2,1,0:T(8,128)}, f32[3,4,8]{2,1,0:T(4,128)}) custom-call(f32[4,1,8,256]{3,2,1,0:T(8,128)S(1)} %get-tuple-element.6.q_ref, f32[3,4,8]{2,1,0:T(4,128)S(1)} %get-tuple-element.7.h_ref), custom_call_target="tpu_custom_call" | custom-call | tf_op jit(solution)/shard_map/pallas_call | solution.py:503

commit v8 on v7

--- a/solution.py
+++ b/solution.py
@@ -64,7 +64,7 @@
 def kernel(
     x_hbm, nb_hbm, rows_hbm, cols_hbm, mirror_hbm, q_ref, h_ref,
     x_ref, nb, rows_ref, cols_ref, mirror_ref,
-    wina, winb, win1, win2, xs, xr, zs, zr, red0, red1, total_ref,
+    wina, winb, win1, win2, xs, xr, zs, zr, red0, red1, total_ref, upper_mask,
     load_sem, swap_send, swap_recv, cross_send, cross_recv, halo_send, halo_recv,
     zx_send, zx_recv, red_send, red_recv, pass_send, pass_recv,
 ):
@@ -258,6 +258,9 @@
     for e in range(NB_DEV):
         nb[e] = jnp.transpose(nb[e])
 
+    for e in range(NB_DEV):
+        upper_mask[e] = jnp.full((NRHS, BLOCK), upper[e], jnp.float32)
+
     def products(windows):
         total = jnp.zeros((16 * len(windows), BLOCK), jnp.float32)
         for e in range(0, NB_DEV, 2):
@@ -266,7 +269,8 @@
                 parts = []
                 for window in windows:
                     picked = window[where_from[f]].astype(jnp.float32)
-                    parts += [picked * upper[f], picked * (1.0 - upper[f])]
+                    first = picked * upper_mask[f]
+                    parts += [first, picked - first]
                 lefts.append(jnp.concatenate(parts, axis=0).astype(jnp.bfloat16))
                 rights.append(nb[f])
             total = total + lax.dot_general(
@@ -481,6 +485,7 @@
             steps, steps,
             *[pltpu.VMEM((size, 1, BLOCK), f32) for size in STAGE_SIZES],
             pltpu.VMEM((1, BLOCK), f32),
+            pltpu.VMEM((NB_DEV, NRHS, BLOCK), f32),
             dma((5,)),
             dma, dma,
             dma, dma,

time: 43.3 us -> 43.3 us (level)
  no operation moved by 1% of the time
where the time goes in v8:
time: 43.3 us; the launch traced here: 43.2 us
  Pallas kernels  42.6 us (98%)
  between operations  0.64 us (1%)
    pallas_call x1, Pallas kernels, on_device(): pl.pallas_call(kernel, out_shape=(jax.ShapeDtypeStruct((ITERS + 1, 1, NRH...  41.9 us

profile of v8, /device:TPU:1, one launch (start us, length us, event | category | flops | bytes accessed | tf_op | source)
XLA Modules:
  0.0 43.2 jit_solution(5589155256057079600)
XLA Ops:
  0.6 41.9 %shard_map.68 = (f32[4,1,8,256]{3,2,1,0:T(8,128)S(1)}, f32[3,4,8]{2,1,0:T(4,128)S(1)}) custom-call(f32[1,8,256]{2,1,0:T(8,128)} %x_hbm.1, bf16[1,32,128,128]{3,2,1,0:T(8,128)(2,1)} %nb_hbm.1, s32[1,32]{1,0:T(1,128)} %rows_hbm.1, s32[1,32]{1,0:T(1,128)} %cols_hbm.1, s32[2,128]{1,0:T(2,128)} %bitcast.2), custom_call_target="tpu_custom_call" | custom-call | tf_op jit(solution)/shard_map/pallas_call | solution.py:469
  42.6 0.6 %shard_map.69 = (f32[4,1,8,256]{3,2,1,0:T(8,128)}, f32[3,4,8]{2,1,0:T(4,128)}) custom-call(f32[4,1,8,256]{3,2,1,0:T(8,128)S(1)} %get-tuple-element.6.q_ref, f32[3,4,8]{2,1,0:T(4,128)S(1)} %get-tuple-element.7.h_ref), custom_call_target="tpu_custom_call" | custom-call | tf_op jit(solution)/shard_map/pallas_call | solution.py:508
